TPU v7x, 512 devices: a whole 4x4x16 slice. The times are simulated.
512 devices in a mesh: dp: 16 (over z), ctx: 32 (over x, y, core).
Axes of the slice: x: 4, y: 4, z: 16, core: 2. Of those that a mesh axis runs over, the one named last changes fastest.
Arguments:
- tokens: bfloat16 [16, 8192, 1024], P('dp', 'ctx'), may hold values from -14 to 14
- w_query: bfloat16 [1024, 1024], replicated, may hold values from -0.1875 to 0.1875
- key_weight: bfloat16 [1024, 256], replicated, may hold values from -0.1875 to 0.1875
- value_weight: bfloat16 [1024, 256], replicated, may hold values from -0.1875 to 0.1875
- cotangent: bfloat16 [16, 8192, 1024], P('dp', 'ctx'), may hold values from -6 to 6
- segment_ids: int32 [16, 8192], P('dp'), may hold values from 0 to 3, never falling along the last dimension, each value on 1 to 4096 neighbouring positions
Outputs:
- grad_inputs: bfloat16 [16, 8192, 1024], P('dp', 'ctx')
- grad_query: float32 [1024, 1024], P('ctx')
- key_weight_gradient: float32 [1024, 256], P('ctx')
- value_weight_gradient: float32 [1024, 256], P('ctx')
Inputs may be any that keep to these rules, and one draw needn't show every extreme that they name: `segment_ids`: along each sequence the document numbers never fall and start at 0; each document has 1 to min(4096, 6144) bytes, and one has exactly that many.
All inputs are finite; a program needn't handle non-finite values.
Results may differ from a plain program's by a relative error of at most 0.014.
The roundings to bfloat16 on the way count: a program that leaves them out, or rounds other values in their place, can miss the bound.
Values may be sent and summed in bfloat16 or wider, within the bound.
A program may use at most 64 MiB of HBM per device.

v0:
```python
import jax
import jax.numpy as jnp
from jax import lax
from jax.sharding import PartitionSpec as P

HEAD_DIMENSION = 128
WINDOW = 1024


NEG_FILL = -1e30


def shifted(block, axis, distance):
    devices = range(lax.axis_size(axis))
    route = [(i - distance, i) for i in devices if i - distance in devices]
    return lax.ppermute(block, axis, route)


def head_terms(
    head_index, q_block, k_block, v_block, c_block, allowed, scale, head_size, group_size
):
    query_group = head_index // group_size
    query = lax.dynamic_slice_in_dim(q_block, head_index * head_size, head_size, 1)
    key_h = lax.dynamic_slice_in_dim(k_block, query_group * head_size, head_size, 1)
    value_h = lax.dynamic_slice_in_dim(v_block, query_group * head_size, head_size, 1)
    dout = lax.dynamic_slice_in_dim(c_block, head_index * head_size, head_size, 1)
    scores = jnp.dot(query, key_h.T, preferred_element_type=jnp.float32) * scale
    scores = jnp.where(allowed, scores, NEG_FILL)
    peak = jnp.max(scores, axis=1, keepdims=True)
    weights = jnp.exp(scores - peak)
    weights = weights / jnp.sum(weights, axis=1, keepdims=True)
    weights_b = weights.astype(jnp.bfloat16)
    attended = jnp.dot(weights_b, value_h, preferred_element_type=jnp.float32)
    delta = jnp.sum(dout.astype(jnp.float32) * attended, axis=1, keepdims=True)
    dprobs = jnp.dot(dout, value_h.T, preferred_element_type=jnp.float32)
    dscores = (weights * (dprobs - delta) * scale).astype(jnp.bfloat16)
    grad_q = jnp.dot(dscores, key_h, preferred_element_type=jnp.float32)
    key_gradient = jnp.dot(dscores.T, query, preferred_element_type=jnp.float32)
    value_gradient = jnp.dot(weights_b.T, dout, preferred_element_type=jnp.float32)
    return (grad_q, key_gradient, value_gradient)


def body(tokens, w_query, key_weight, value_weight, cotangent, segment_ids):
    sequence = tokens[0]
    cot = cotangent[0]
    seg = segment_ids[0]
    rows = sequence.shape[0]
    q_cols = w_query.shape[1]
    key_value_columns = key_weight.shape[1]
    head_size = HEAD_DIMENSION
    heads = q_cols // head_size
    kv_heads = key_value_columns // head_size
    group_size = heads // kv_heads
    reach = WINDOW // rows
    column_width = (reach + 1) * rows
    scale = head_size ** (-0.5)
    position = lax.axis_index("ctx")
    start = position * rows
    queries = jnp.dot(sequence, w_query, preferred_element_type=jnp.float32).astype(jnp.bfloat16)
    keys = jnp.dot(sequence, key_weight, preferred_element_type=jnp.float32).astype(jnp.bfloat16)
    values = jnp.dot(sequence, value_weight, preferred_element_type=jnp.float32).astype(
        jnp.bfloat16
    )
    earlier = [shifted((keys, values), "ctx", reach - slot) for slot in range(reach)]
    k_block = jnp.concatenate([pair[0] for pair in earlier] + [keys], axis=0)
    v_block = jnp.concatenate([pair[1] for pair in earlier] + [values], axis=0)
    seg_pad = jnp.concatenate([-jnp.ones((WINDOW,), jnp.int32), seg], axis=0)
    q_seg = lax.dynamic_slice_in_dim(seg, start, rows, 0)
    k_seg = lax.dynamic_slice_in_dim(seg_pad, start, column_width, 0)
    q_pos = start + jnp.arange(rows, dtype=jnp.int32)
    k_pos = start - reach * rows + jnp.arange(column_width, dtype=jnp.int32)
    gap = q_pos[:, None] - k_pos[None, :]
    allowed = (
        (gap >= 0) & (gap < WINDOW) & (k_pos[None, :] >= 0) & (q_seg[:, None] == k_seg[None, :])
    )
    grad_q, key_gradient, value_gradient = lax.map(
        lambda head_index: head_terms(
            head_index, queries, k_block, v_block, cot, allowed, scale, head_size, group_size
        ),
        jnp.arange(heads, dtype=jnp.int32),
    )
    dq_local = grad_q.transpose(1, 0, 2).reshape(rows, q_cols).astype(jnp.bfloat16)
    dk_local = (
        key_gradient.reshape(kv_heads, group_size, column_width, head_size)
        .sum(axis=1)
        .transpose(1, 0, 2)
        .reshape(column_width, key_value_columns)
    )
    dv_local = (
        value_gradient.reshape(kv_heads, group_size, column_width, head_size)
        .sum(axis=1)
        .transpose(1, 0, 2)
        .reshape(column_width, key_value_columns)
    )

    def piece(distance):
        first = (reach - distance) * rows
        return (dk_local[first : first + rows], dv_local[first : first + rows])

    dk_total, dv_total = piece(0)
    for distance in range(1, reach + 1):
        got_k, got_v = shifted(piece(distance), "ctx", -distance)
        dk_total = dk_total + got_k
        dv_total = dv_total + got_v
    dk_b = dk_total.astype(jnp.bfloat16)
    dv_b = dv_total.astype(jnp.bfloat16)
    grad_in = (
        jnp.dot(dq_local, w_query.T, preferred_element_type=jnp.float32)
        + jnp.dot(dk_b, key_weight.T, preferred_element_type=jnp.float32)
        + jnp.dot(dv_b, value_weight.T, preferred_element_type=jnp.float32)
    ).astype(jnp.bfloat16)
    combined = jnp.concatenate([dq_local, dk_b, dv_b], axis=1)
    partial_value = lax.dot_general(
        sequence, combined, (((0,), (0,)), ((), ())), preferred_element_type=jnp.float32
    )
    summed = lax.psum_scatter(
        lax.optimization_barrier(partial_value.astype(jnp.bfloat16))
        .astype(jnp.float32)
        .astype(jnp.bfloat16),
        "ctx",
        scatter_dimension=0,
        tiled=True,
    ).astype(jnp.float32)
    summed = lax.psum(summed, "dp")
    norm_factor = (lax.axis_size("dp") * lax.axis_size("ctx") * rows) ** (-0.5)
    summed = summed * norm_factor
    grad_query = summed[:, :q_cols]
    key_weight_gradient = summed[:, q_cols : q_cols + key_value_columns]
    value_weight_gradient = summed[:, q_cols + key_value_columns :]
    return (grad_in[None], grad_query, key_weight_gradient, value_weight_gradient)


def solution(mesh):
    placed = (P("dp", "ctx", None), P(), P(), P(), P("dp", "ctx", None), P("dp", None))
    return jax.shard_map(
        body,
        mesh=mesh,
        in_specs=placed,
        out_specs=(P("dp", "ctx", None), P("ctx", None), P("ctx", None), P("ctx", None)),
        check_vma=False,
    )
```

profile of v0, /device:TPU:24, one launch (start us, length us, event | category | flops | bytes accessed | tf_op | source)
XLA Modules:
  0.0 429.7 jit_solution(338459970549987686)
XLA Ops:
  10.8 3.1 collective-permute-start.6
  13.9 4.5 %collective-permute-start.5 = (bf16[256,256]{1,0:T(8,128)(2,1)S(1)}, bf16[256,256]{1,0:T(8,128)(2,1)}, u32[]{:S(2)}, u32[]{:S(2)}) collective-permute-start(bf16[256,256]{1,0:T(8,128)(2,1)S(1)} %convolution_convert_fusion.2), channel_id=1, source_target_pairs={{0,3},{1,4},{2,5},{3,6},{4,7},{5,8},{6,9},{7,10},{8,11},{9,12},{10... | collective-permute-start | bytes 393224 | tf_op jit(solution)/shard_map/ppermute | solution.py:16
  19.9 3.5 collective-permute-start.1
  23.4 2.9 collective-permute-start
  33.3 4.0 collective-permute-start.2
  41.4 3.7 collective-permute-start.4
  45.2 5.9 %collective-permute-done.4 = bf16[256,256]{1,0:T(8,128)(2,1)S(1)} collective-permute-done((bf16[256,256]{1,0:T(8,128)(2,1)S(1)}, bf16[256,256]{1,0:T(8,128)(2,1)S(1)}, u32[]{:S(2)}, u32[]{:S(2)}) %collective-permute-start.4) | collective-permute-done | bytes 131104 | tf_op jit(solution)/shard_map/ppermute | solution.py:16
  54.7 116.8 %while.17 = (s32[]{:T(128)}, bf16[8,256,128]{1,2,0:T(8,128)(2,1)}, f32[8,1280,128]{2,1,0:T(8,128)}, f32[8,1280,128]{2,1,0:T(8,128)}, s32[8]{0:T(128)S(1)}, /*ind...) while((s32[]{:T(128)}, bf16[8,256,128]{1,2,0:T(8,128)(2,1)}, ...), condition=%wide.region_4.5_spmd.clone, body=%wide.region_0.4_spmd.clone.sunk | while | flops 511278368 | bytes 14253591 | solution.py:76
  65.0 2.2 fusion.103
  79.6 2.2 fusion.103
  94.2 2.2 fusion.103
  108.8 2.2 fusion.103
  123.3 2.3 fusion.103
  138.0 2.3 fusion.103
  152.6 2.2 fusion.103
  167.2 2.2 fusion.103
  171.5 2.9 bitcast_reduce_fusion
  188.3 2.9 bitcast_reduce_fusion.1
  200.3 2.1 collective-permute-start.9
  210.0 21.9 %collective-permute-done.9 = f32[256,256]{0,1:T(8,128)} collective-permute-done((f32[256,256]{0,1:T(8,128)}, f32[256,256]{0,1:T(8,128)}, u32[]{:S(2)}, u32[]{:S(2)}) %collective-permute-start.9) | collective-permute-done | bytes 262176 | tf_op jit(solution)/shard_map/ppermute | solution.py:16
  233.3 2.7 fusion.33
  235.9 4.7 %copy.39 = bf16[1024,1536]{1,0:T(8,128)(2,1)} copy(bf16[1024,1536]{0,1:T(8,128)(2,1)} %fusion.33) | data formatting | bytes 6291456
  244.8 108.5 %reduce-scatter.4.cloned.1.call-done = bf16[32,1536]{1,0:T(8,128)(2,1)} async-done(((bf16[1024,1536]{1,0:T(8,128)(2,1)}), bf16[32,1536]{1,0:T(8,128)(2,1)}) %reduce-scatter.4.cloned.1.call-update) | async-done | bytes 98320
  354.5 66.0 %all-reduce.2 = f32[32,1536]{0,1:T(8,128)S(1)} all-reduce(bf16[32,1536]{0,1:T(8,128)(2,1)S(1)} %copy.40), channel_id=1, replica_groups=mesh['dp'=16,'ctx'=32] {'dp'}, use_global_device_ids=true, to_apply=%region_8.9 | all-reduce | flops 49152 | bytes 294912 | tf_op jit(solution)/shard_map/psum | solution.py:124
  (167 shorter events, 132.0 us)
Async XLA Ops:
  7.2 19.7 %copy-start = (bf16[1024,1024]{1,0:T(8,128)(2,1)S(1)}, bf16[1024,1024]{1,0:T(8,128)(2,1)}, u32[]{:S(2)}) copy-start(bf16[1024,1024]{1,0:T(8,128)(2,1)} %param.9) | copy-start | bytes 6291460
  7.2 19.7 %copy-start.2 = (bf16[1,256,1024]{2,1,0:T(8,128)(2,1)S(1)}, bf16[1,256,1024]{2,1,0:T(8,128)(2,1)}, u32[]{:S(2)}) copy-start(bf16[1,256,1024]{2,1,0:T(8,128)(2,1)} %param.8) | copy-start | bytes 1572868
  7.2 346.2 %reduce-scatter.4.cloned.1.call-start = ((), (), s32[]{:S(2)}) async-start(), calls=%async_computation.1 | async-start | bytes 3244032
  8.9 44.0 %collective-permute-start.7 = (bf16[256,256]{1,0:T(8,128)(2,1)S(1)}, bf16[256,256]{1,0:T(8,128)(2,1)}, u32[]{:S(2)}, u32[]{:S(2)}) collective-permute-start(bf16[256,256]{1,0:T(8,128)(2,1)S(1)} %convolution_convert_fusion.2), channel_id=1, source_target_pairs={{0,1},{1,2},{2,3},{3,4},{4,5},{5,6},{6,7},{7,8},{8,9},{9,10},{10,1... | collective-permute-start | bytes 393224 | tf_op jit(solution)/shard_map/ppermute | solution.py:16
  10.8 41.2 %collective-permute-start.6 = (bf16[256,256]{1,0:T(8,128)(2,1)S(1)}, bf16[256,256]{1,0:T(8,128)(2,1)}, u32[]{:S(2)}, u32[]{:S(2)}) collective-permute-start(bf16[256,256]{1,0:T(8,128)(2,1)S(1)} %convolution_convert_fusion.2), channel_id=1, source_target_pairs={{0,2},{1,3},{2,4},{3,5},{4,6},{5,7},{6,8},{7,9},{8,10},{9,11},{10,... | collective-permute-start | bytes 393224 | tf_op jit(solution)/shard_map/ppermute | solution.py:16
  13.9 37.2 %collective-permute-start.5 = (bf16[256,256]{1,0:T(8,128)(2,1)S(1)}, bf16[256,256]{1,0:T(8,128)(2,1)}, u32[]{:S(2)}, u32[]{:S(2)}) collective-permute-start(bf16[256,256]{1,0:T(8,128)(2,1)S(1)} %convolution_convert_fusion.2), channel_id=1, source_target_pairs={{0,3},{1,4},{2,5},{3,6},{4,7},{5,8},{6,9},{7,10},{8,11},{9,12},{10... | collective-permute-start | bytes 393224 | tf_op jit(solution)/shard_map/ppermute | solution.py:16
  19.9 18.3 %collective-permute-start.1 = (bf16[256,256]{1,0:T(8,128)(2,1)S(1)}, bf16[256,256]{1,0:T(8,128)(2,1)}, u32[]{:S(2)}, u32[]{:S(2)}) collective-permute-start(bf16[256,256]{1,0:T(8,128)(2,1)S(1)} %convolution_convert_fusion.3), channel_id=1, source_target_pairs={{0,3},{1,4},{2,5},{3,6},{4,7},{5,8},{6,9},{7,10},{8,11},{9,12},{10... | collective-permute-start | bytes 393224 | tf_op jit(solution)/shard_map/ppermute | solution.py:16
  23.4 9.2 %collective-permute-start = (bf16[256,256]{1,0:T(8,128)(2,1)S(1)}, bf16[256,256]{1,0:T(8,128)(2,1)S(1)}, u32[]{:S(2)}, u32[]{:S(2)}) collective-permute-start(bf16[256,256]{1,0:T(8,128)(2,1)S(1)} %convolution_convert_fusion.3), channel_id=1, source_target_pairs={{0,4},{1,5},{2,6},{3,7},{4,8},{5,9},{6,10},{7,11},{8,12},{9,13},{1... | collective-permute-start | bytes 393224 | tf_op jit(solution)/shard_map/ppermute | solution.py:16
  26.9 4.1 copy-start.6
  33.3 8.1 %collective-permute-start.2 = (bf16[256,256]{1,0:T(8,128)(2,1)S(1)}, bf16[256,256]{1,0:T(8,128)(2,1)S(1)}, u32[]{:S(2)}, u32[]{:S(2)}) collective-permute-start(bf16[256,256]{1,0:T(8,128)(2,1)S(1)} %convolution_convert_fusion.3), channel_id=1, source_target_pairs={{0,2},{1,3},{2,4},{3,5},{4,6},{5,7},{6,8},{7,9},{8,10},{9,11},{10,... | collective-permute-start | bytes 393224 | tf_op jit(solution)/shard_map/ppermute | solution.py:16
  38.2 6.9 %collective-permute-start.3 = (bf16[256,256]{1,0:T(8,128)(2,1)S(1)}, bf16[256,256]{1,0:T(8,128)(2,1)S(1)}, u32[]{:S(2)}, u32[]{:S(2)}) collective-permute-start(bf16[256,256]{1,0:T(8,128)(2,1)S(1)} %convolution_convert_fusion.3), channel_id=1, source_target_pairs={{0,1},{1,2},{2,3},{3,4},{4,5},{5,6},{6,7},{7,8},{8,9},{9,10},{10,1... | collective-permute-start | bytes 393224 | tf_op jit(solution)/shard_map/ppermute | solution.py:16
  41.4 9.6 %collective-permute-start.4 = (bf16[256,256]{1,0:T(8,128)(2,1)S(1)}, bf16[256,256]{1,0:T(8,128)(2,1)S(1)}, u32[]{:S(2)}, u32[]{:S(2)}) collective-permute-start(bf16[256,256]{1,0:T(8,128)(2,1)S(1)} %convolution_convert_fusion.2), channel_id=1, source_target_pairs={{0,4},{1,5},{2,6},{3,7},{4,8},{5,9},{6,10},{7,11},{8,12},{9,13},{1... | collective-permute-start | bytes 393224 | tf_op jit(solution)/shard_map/ppermute | solution.py:16
  45.2 9.6 %copy-start.10 = (pred[1280]{0:T(1024)(128)(4,1)S(1)}, pred[1280]{0:T(1024)(128)(4,1)}, u32[]{:S(2)}) copy-start(pred[1280]{0:T(1024)(128)(4,1)} %broadcast_compare_fusion) | copy-start | bytes 3844
  45.2 9.6 %copy-start.11 = (s32[1,256]{1,0:T(1,128)S(1)}, s32[1,256]{1,0:T(1,128)}, u32[]{:S(2)}) copy-start(s32[1,256]{1,0:T(1,128)} %constant_dynamic-slice_fusion) | copy-start | bytes 3076
  45.2 9.5 %copy-start.12 = (s32[256]{0:T(256)S(1)}, s32[256]{0:T(256)}, u32[]{:S(2)}) copy-start(s32[256]{0:T(256)} %iota_add_fusion.1) | copy-start | bytes 3076
  180.6 19.7 %collective-permute-start.12 = (f32[256,256]{0,1:T(8,128)}, f32[256,256]{0,1:T(8,128)}, u32[]{:S(2)}, u32[]{:S(2)}) collective-permute-start(f32[256,256]{0,1:T(8,128)} %bitcast.16), channel_id=1, source_target_pairs={{1,0},{2,1},{3,2},{4,3},{5,4},{6,5},{7,6},{8,7},{9,8},{10,9},{11,1... | collective-permute-start | bytes 786440 | tf_op jit(solution)/shard_map/ppermute | solution.py:16
  182.5 20.1 %collective-permute-start.13 = (f32[256,256]{0,1:T(8,128)}, f32[256,256]{0,1:T(8,128)}, u32[]{:S(2)}, u32[]{:S(2)}) collective-permute-start(f32[256,256]{0,1:T(8,128)} %bitcast.101), channel_id=1, source_target_pairs={{2,0},{3,1},{4,2},{5,3},{6,4},{7,5},{8,6},{9,7},{10,8},{11,9},{12,... | collective-permute-start | bytes 786440 | tf_op jit(solution)/shard_map/ppermute | solution.py:16
  184.4 22.1 %collective-permute-start.14 = (f32[256,256]{0,1:T(8,128)}, f32[256,256]{0,1:T(8,128)}, u32[]{:S(2)}, u32[]{:S(2)}) collective-permute-start(f32[256,256]{0,1:T(8,128)} %bitcast.98), channel_id=1, source_target_pairs={{3,0},{4,1},{5,2},{6,3},{7,4},{8,5},{9,6},{10,7},{11,8},{12,9},{13... | collective-permute-start | bytes 786440 | tf_op jit(solution)/shard_map/ppermute | solution.py:16
  186.4 22.3 %collective-permute-start.15 = (f32[256,256]{0,1:T(8,128)}, f32[256,256]{0,1:T(8,128)}, u32[]{:S(2)}, u32[]{:S(2)}) collective-permute-start(f32[256,256]{0,1:T(8,128)} %bitcast.96), channel_id=1, source_target_pairs={{4,0},{5,1},{6,2},{7,3},{8,4},{9,5},{10,6},{11,7},{12,8},{13,9},{1... | collective-permute-start | bytes 786440 | tf_op jit(solution)/shard_map/ppermute | solution.py:16
  198.3 11.7 %collective-permute-start.8 = (f32[256,256]{0,1:T(8,128)}, f32[256,256]{0,1:T(8,128)}, u32[]{:S(2)}, u32[]{:S(2)}) collective-permute-start(f32[256,256]{0,1:T(8,128)} %bitcast.102), channel_id=1, source_target_pairs={{1,0},{2,1},{3,2},{4,3},{5,4},{6,5},{7,6},{8,7},{9,8},{10,9},{11,1... | collective-permute-start | bytes 786440 | tf_op jit(solution)/shard_map/ppermute | solution.py:16
  200.3 31.7 %collective-permute-start.9 = (f32[256,256]{0,1:T(8,128)}, f32[256,256]{0,1:T(8,128)}, u32[]{:S(2)}, u32[]{:S(2)}) collective-permute-start(f32[256,256]{0,1:T(8,128)} %bitcast.100), channel_id=1, source_target_pairs={{2,0},{3,1},{4,2},{5,3},{6,4},{7,5},{8,6},{9,7},{10,8},{11,9},{12,... | collective-permute-start | bytes 786440 | tf_op jit(solution)/shard_map/ppermute | solution.py:16
  202.6 29.4 %collective-permute-start.10 = (f32[256,256]{0,1:T(8,128)}, f32[256,256]{0,1:T(8,128)}, u32[]{:S(2)}, u32[]{:S(2)}) collective-permute-start(f32[256,256]{0,1:T(8,128)} %bitcast.99), channel_id=1, source_target_pairs={{3,0},{4,1},{5,2},{6,3},{7,4},{8,5},{9,6},{10,7},{11,8},{12,9},{13... | collective-permute-start | bytes 786440 | tf_op jit(solution)/shard_map/ppermute | solution.py:16
  206.5 25.5 %collective-permute-start.11 = (f32[256,256]{0,1:T(8,128)}, f32[256,256]{0,1:T(8,128)}, u32[]{:S(2)}, u32[]{:S(2)}) collective-permute-start(f32[256,256]{0,1:T(8,128)} %bitcast.97), channel_id=1, source_target_pairs={{4,0},{5,1},{6,2},{7,3},{8,4},{9,5},{10,6},{11,7},{12,8},{13,9},{1... | collective-permute-start | bytes 786440 | tf_op jit(solution)/shard_map/ppermute | solution.py:16
  208.7 24.5 %copy-start.4 = (bf16[8,256,128]{1,2,0:T(8,128)(2,1)S(1)}, bf16[8,256,128]{1,2,0:T(8,128)(2,1)}, u32[]{:S(2)}) copy-start(bf16[8,256,128]{1,2,0:T(8,128)(2,1)} %get-tuple-element.132) | copy-start | bytes 1572868
  (13 other events, 13.4 us)
Sparse Core Ops, SparseCore 0:
  240.7 112.6 reduce-scatter.3
where the time goes:
time: 434 us; the launch traced here: 430 us
  waiting for transfers between devices  140 us (32%)
  matrix products  86.7 us (20%)
  blocking collectives  66 us (15%)
  local copies, waits for them, and re-layouts  42.5 us (10%)
  starting transfers between devices  41.1 us (9%)
  loops' own time  26.3 us (6%)
  between operations  14.5 us (3%)
  other arithmetic  13.1 us (3%)
    unnamed x2, waiting for transfers between devices  109 us
    psum x1, blocking collectives, body(): summed = lax.psum(summed, 'dp')  66 us
    ppermute x16, starting transfers between devices, shifted(): return lax.ppermute(block, axis, route)  41.1 us
    ppermute x16, waiting for transfers between devices, shifted(): return lax.ppermute(block, axis, route)  31 us
    another operation x1, loops' own time, body(): lax.map(lambda head_index: head_terms(head_index, queries, k_block, v_blo...  26.3 us
    dot_general x8, matrix products, head_terms(): jnp.dot(weights_b.T, dout, preferred_element_type=jnp.float32)  17.7 us
    unnamed x38, local copies, waits for them, and re-layouts  17.1 us
    dot_general x8, matrix products, head_terms(): key_gradient = jnp.dot(dscores.T, query, preferred_element_type=jnp.float32)  16.6 us
  transfers between devices with their start and end apart: 17, of which 7 were waited for; matrix products, arithmetic and copies ran while one was open for 6% of the time, Pallas kernels for 0%

commit v1 on v0

v1 whole, which is shorter than its diff:
```python
import functools
import math

import jax
import jax.numpy as jnp
from jax import lax
from jax.experimental import pallas as pl
from jax.experimental.pallas import tpu as pltpu
from jax.sharding import PartitionSpec as P

HEAD = 128
WINDOW = 1024
NEG = -1e30
BF = jnp.bfloat16
F32 = jnp.float32
MESH = pl.DeviceIdType.MESH


def nn(a, b):
    return lax.dot_general(a, b, (((1,), (0,)), ((), ())), preferred_element_type=F32)


def nt(a, b):
    return lax.dot_general(a, b, (((1,), (1,)), ((), ())), preferred_element_type=F32)


def tn(a, b):
    return lax.dot_general(a, b, (((0,), (0,)), ((), ())), preferred_element_type=F32)


class Plan:
    def __init__(self, sizes, rows, width, q_cols, kv_cols, length):
        self.Z, self.N = sizes["dp"], sizes["ctx"]
        self.X = self.Y = math.isqrt(self.N // 2)
        self.rows, self.width, self.q_cols, self.kv_cols = rows, width, q_cols, kv_cols
        self.length = length
        self.heads = q_cols // HEAD
        self.groups = kv_cols // HEAD
        self.per = self.heads // self.groups
        self.reach = WINDOW // rows
        self.chips = self.N // 2
        self.own = width // self.N
        half = q_cols // 2
        self.q_pieces = ((0, half, True), (half, half, False))
        self.kv_pieces = ((q_cols, kv_cols, True), (q_cols + kv_cols, kv_cols, False))
        self.parts = (self.q_pieces, self.kv_pieces)
        self.scratch = {}
        self.sems = {}

    def buf(self, name, shape, dtype):
        self.scratch[name] = pltpu.VMEM(shape, dtype)

    def sem(self, name, *shape):
        self.sems[name] = pltpu.SemaphoreType.DMA(shape)


def build_plan(sizes, rows, width, q_cols, kv_cols, length):
    p = Plan(sizes, rows, width, q_cols, kv_cols, length)
    lanes = p.per * rows
    blocks = p.reach + 1
    p.buf("tok", (rows, width), BF)
    p.buf("wq", (width, q_cols), BF)
    p.buf("wk", (width, kv_cols), BF)
    p.buf("wv", (width, kv_cols), BF)
    p.buf("cot", (rows, q_cols), BF)
    p.buf("seg", (1, length), jnp.int32)
    p.buf("kvb", (blocks, 2 * p.groups, rows, HEAD), BF)
    p.buf("qst", (p.groups, lanes, HEAD), BF)
    p.buf("dost", (p.groups, lanes, HEAD), BF)
    p.buf("bias", (blocks, rows, rows), F32)
    p.buf("s", (p.groups, blocks, rows, lanes), F32)
    p.buf("dp", (p.groups, blocks, rows, lanes), F32)
    p.buf("m", (p.groups, 8, lanes), F32)
    p.buf("l", (8, lanes), F32)
    p.buf("de", (8, lanes), F32)
    p.buf("acc", (p.groups, blocks, 2, rows, HEAD), F32)
    p.buf("dqt", (HEAD, lanes), F32)
    p.buf("stage", (p.groups, blocks, 2, rows, HEAD), BF)
    p.buf("back", (p.groups, blocks, 2, rows, HEAD), BF)
    p.buf("tokt", (2, width // 2, rows), BF)
    p.buf("toktp", (width // 2, rows), BF)
    p.buf("dq", (rows, q_cols), BF)
    p.buf("dqp", (rows, q_cols), BF)
    p.buf("dkv", (2, rows, kv_cols), BF)
    p.buf("dkvp", (2, rows, kv_cols), BF)
    p.buf("gi32", (rows, width), F32)
    p.buf("gi", (rows, width), BF)
    own, R = p.own, p.X
    for i, part in enumerate(p.parts):
        for j, (first, cols, x_first) in enumerate(part):
            p.buf(f"one{i}{j}", (R, R * own, cols), BF)
            p.buf(f"got{i}{j}", (R - 1, R * own, cols), BF)
            p.buf(f"two{i}{j}", (R, own, cols), BF)
            p.buf(f"gat{i}{j}", (R - 1, own, cols), BF)
            p.sem(f"one{i}{j}", 2, R)
            p.sem(f"two{i}{j}", 2, R)
        tiles = own // 8 * sum(c for _, c, _ in part) // HEAD
        p.buf(f"zs{i}", (p.Z, tiles // p.Z * 8, HEAD), F32)
        p.buf(f"zr{i}", (p.Z, tiles // p.Z * 8, HEAD), F32)
        p.buf(f"zo{i}", (p.Z, tiles // p.Z * 8, HEAD), F32)
        p.sem(f"zr{i}", 2, p.Z)
        p.sem(f"zo{i}", 2, p.Z)
    p.sem("load", 6)
    p.sem("out")
    p.sem("halo", 2, 4)
    p.sem("tokt", 2)
    p.sem("dq", 2)
    p.sem("dkv", 2)
    p.sem("ret", 2, p.groups, blocks)
    return p


def kernel(p, tok_h, wq_h, wk_h, wv_h, cot_h, seg_h, gi_h, gq_ref, gk_ref, gv_ref, *refs):
    names = list(p.scratch)
    r = dict(zip(names, refs[: len(names)]))
    sm = dict(zip(p.sems, refs[len(names) :]))
    rows, lanes, blocks = p.rows, p.per * p.rows, p.reach + 1
    X, Y, Z, N, R = p.X, p.Y, p.Z, p.N, p.X
    z, me = lax.axis_index("dp"), lax.axis_index("ctx")
    core, chip = lax.rem(me, 2), me // 2
    cx, cy = chip // Y, lax.rem(chip, Y)
    peer = me + 1 - 2 * core
    nxt, prv = lax.rem(me + 2, N), lax.rem(me + N - 2, N)
    scale = HEAD**-0.5

    def along_x(o):
        return (lax.rem(cx + o, X) * Y + cy) * 2 + core

    def along_y(o):
        return (cx * Y + lax.rem(cy + o, Y)) * 2 + core

    def remote(src, dst, send, recv, ctx, dp=None):
        return pltpu.make_async_remote_copy(
            src_ref=src, dst_ref=dst, send_sem=send, recv_sem=recv,
            device_id=(z if dp is None else dp, ctx), device_id_type=MESH,
        )

    loads = {}
    for i, (name, src) in enumerate(
        (("tok", tok_h), ("wk", wk_h), ("wv", wv_h), ("wq", wq_h), ("cot", cot_h), ("seg", seg_h))
    ):
        loads[name] = pltpu.make_async_copy(src, r[name], sm["load"].at[i])
        loads[name].start()
    barrier = pltpu.get_barrier_semaphore()

    def greet(ctx, dp):
        pl.semaphore_signal(barrier, inc=1, device_id=(dp, ctx), device_id_type=MESH)

    def greet_z(o, c):
        greet(me, lax.rem(z + o, Z))
        return c

    lax.fori_loop(1, Z, greet_z, 0)
    for d in [peer, nxt, prv] + [along_x(o) for o in range(1, X)] + [along_y(o) for o in range(1, Y)]:
        greet(d, z)

    for name in ("tok", "wk", "wv"):
        loads[name].wait()
    for i, w in enumerate(("wk", "wv")):
        val = nn(r["tok"][...], r[w][...]).astype(BF)
        for g in range(p.groups):
            r["kvb"][0, i * p.groups + g] = val[:, g * HEAD : (g + 1) * HEAD]
    pl.semaphore_wait(barrier, 3 + (X - 1) + (Y - 1) + (Z - 1))

    kvb = r["kvb"]

    def halo(k, src, dst, to):
        return remote(kvb.at[src], kvb.at[dst], sm["halo"].at[0, k], sm["halo"].at[1, k], to)

    halo(0, 0, 2, nxt).start()

    @pl.when(core == 0)
    def _():
        halo(1, 0, 1, peer).start()

    loads["wq"].wait()
    step = 2 * HEAD
    for n in range(p.q_cols // step):
        val = nn(r["tok"][...], r["wq"][:, n * step : (n + 1) * step]).astype(BF)
        for j in range(2):
            g, h = divmod(2 * n + j, p.per)
            r["qst"][g, h * rows : (h + 1) * rows] = val[:, j * HEAD : (j + 1) * HEAD]
    loads["cot"].wait()
    for n in range(p.heads):
        g, h = divmod(n, p.per)
        r["dost"][g, h * rows : (h + 1) * rows] = r["cot"][:, n * HEAD : (n + 1) * HEAD]

    loads["seg"].wait()
    start = me * rows
    seg = r["seg"][...]
    q_seg = r["seg"][:, pl.ds(pl.multiple_of(start, rows), rows)]
    doc = jnp.zeros((1, rows), jnp.int32)
    for t in range(1, 4):
        below = jnp.sum((seg < t).astype(F32), axis=1, keepdims=True)
        doc = jnp.where(q_seg >= t, below.astype(jnp.int32), doc)
    row = lax.broadcasted_iota(jnp.int32, (rows, rows), 0)
    col = lax.broadcasted_iota(jnp.int32, (rows, rows), 1)
    for b in range(blocks):
        j = row + (start - b * rows)
        gap = col - row + b * rows
        ok = (j >= doc) & (gap >= 0) & (gap < WINDOW)
        r["bias"][b] = jnp.where(ok, 0.0, NEG)

    for n in range(p.width // HEAD):
        val = r["tok"][:, n * HEAD : (n + 1) * HEAD].astype(F32).T.astype(BF)
        for k in range(HEAD // p.own):
            ch, c = divmod(n * (HEAD // p.own) + k, 2)
            r["tokt"][c, ch * p.own : (ch + 1) * p.own] = val[k * p.own : (k + 1) * p.own]
    tokt_copy = remote(r["tokt"].at[1 - core], r["toktp"], sm["tokt"].at[0], sm["tokt"].at[1], peer)
    tokt_copy.start()

    r["m"][...] = jnp.full(r["m"].shape, -3e38, F32)

    def pass1(b):
        def body(g, c):
            kk, vv = kvb[b, g], kvb[b, p.groups + g]
            for h in range(p.per):
                cols = slice(h * rows, (h + 1) * rows)
                s = nt(kk, r["qst"][g, cols]) + r["bias"][b]
                r["s"][g, b, :, cols] = s
                r["m"][g, :, cols] = jnp.maximum(
                    r["m"][g, :, cols], jnp.max(s.reshape(rows // 8, 8, rows), axis=0)
                )
                r["dp"][g, b, :, cols] = nt(vv, r["dost"][g, cols])
            return c

        lax.fori_loop(0, p.groups, body, 0)

    pass1(0)
    halo(0, 0, 2, nxt).wait_recv()
    halo(2, 2, 4, nxt).start()

    @pl.when(core == 0)
    def _():
        halo(3, 2, 3, peer).start()

    @pl.when(core == 1)
    def _():
        halo(1, 2, 1, peer).start()

    pass1(2)
    halo(1, 0, 1, peer).wait_recv()
    pass1(1)
    halo(2, 2, 4, nxt).wait_recv()

    @pl.when(core == 1)
    def _():
        halo(3, 4, 3, peer).start()

    pass1(4)
    halo(3, 2, 3, peer).wait_recv()
    pass1(3)

    acc, stage, back = r["acc"], r["stage"], r["back"]
    first_core = (core == 0).astype(F32)
    second_core = (core == 1).astype(F32)

    def ret(g, d, to):
        return remote(stage.at[g, d], back.at[g, d], sm["ret"].at[0, g, d], sm["ret"].at[1, g, d], to)

    def pass2(g):
        m = jnp.max(r["m"][g], axis=0, keepdims=True)
        r["m"][g, 0:1] = m
        r["l"][...] = jnp.zeros(r["l"].shape, F32)
        r["de"][...] = jnp.zeros(r["de"].shape, F32)

        def expo(b, c):
            for h in range(p.per):
                cols = slice(h * rows, (h + 1) * rows)
                e = jnp.exp((r["s"][g, b, :, cols] - r["m"][g, 0:1, cols]) * scale)
                r["s"][g, b, :, cols] = e
                r["l"][:, cols] += jnp.sum(e.reshape(rows // 8, 8, rows), axis=0)
                de = e * r["dp"][g, b, :, cols]
                r["de"][:, cols] += jnp.sum(de.reshape(rows // 8, 8, rows), axis=0)
            return c

        lax.fori_loop(0, blocks, expo, 0)
        inv = 1.0 / jnp.sum(r["l"][...], axis=0, keepdims=True)
        delta = jnp.sum(r["de"][...], axis=0, keepdims=True) * inv
        r["l"][0:1] = inv
        r["de"][0:1] = delta
        r["dqt"][...] = jnp.zeros(r["dqt"].shape, F32)

        def grads(t, c):
            b = lax.rem(3 + 3 * t, blocks) if blocks == 5 else t
            kk = kvb[b, g]
            dv = jnp.zeros((rows, HEAD), F32)
            dk = jnp.zeros((rows, HEAD), F32)
            for h in range(p.per):
                cols = slice(h * rows, (h + 1) * rows)
                prob = r["s"][g, b, :, cols] * r["l"][0:1, cols]
                ds = (prob * (r["dp"][g, b, :, cols] - r["de"][0:1, cols]) * scale).astype(BF)
                dv = dv + nn(prob.astype(BF), r["dost"][g, cols])
                dk = dk + nn(ds, r["qst"][g, cols])
                r["dqt"][:, cols] += tn(kk, ds)
            acc[g, b, 0] = dk
            acc[g, b, 1] = dv
            stage[g, b, 0] = dk.astype(BF)
            stage[g, b, 1] = dv.astype(BF)
            return c

        lax.fori_loop(0, blocks, grads, 0)
        ret(g, 3, peer).start()
        ret(g, 1, peer).start()
        for h in range(p.per):
            n = g * p.per + h
            r["dq"][:, n * HEAD : (n + 1) * HEAD] = r["dqt"][:, h * rows : (h + 1) * rows].T.astype(BF)

    def ret4(g):
        ret(g, 3, peer).wait_recv()
        ret(g, 1, peer).wait_recv()
        stage[g, 4] = (acc[g, 4] + second_core * back[g, 3].astype(F32)).astype(BF)
        ret(g, 4, prv).start()

    def ret2(g):
        ret(g, 4, prv).wait_recv()
        t = acc[g, 2] + back[g, 4].astype(F32)
        t = t + first_core * back[g, 3].astype(F32) + second_core * back[g, 1].astype(F32)
        stage[g, 2] = t.astype(BF)
        ret(g, 2, prv).start()

    def ret0(g):
        ret(g, 2, prv).wait_recv()
        t = acc[g, 0] + back[g, 2].astype(F32) + first_core * back[g, 1].astype(F32)
        for i in range(2):
            r["dkv"][i, :, g * HEAD : (g + 1) * HEAD] = t[i].astype(BF)

    def made(i, grads):
        for j, (first, cols, x_first) in enumerate(p.parts[i]):
            mine, other = grads(j)
            one = r[f"one{i}{j}"]

            def block(a, c, mine=mine, other=other, one=one, x_first=x_first):
                at = pl.ds(pl.multiple_of(a * (Y * p.own), Y * p.own), Y * p.own)
                val = nn(r["tokt"][core, at], mine()) + nn(r["toktp"][at], other())
                val = val.astype(BF)
                if x_first:
                    one[a] = val
                else:
                    for k in range(Y):
                        one[k, pl.ds(pl.multiple_of(a * p.own, p.own), p.own)] = val[k * p.own : (k + 1) * p.own]
                return c

            lax.fori_loop(0, X, block, 0)

    def first_hop(i, j, o, x_first):
        at = lax.rem((cx if x_first else cy) + o, R)
        to = along_x(o) if x_first else along_y(o)
        s = sm[f"one{i}{j}"]
        return remote(r[f"one{i}{j}"].at[at], r[f"got{i}{j}"].at[o - 1], s.at[0, o], s.at[1, o], to)

    def second_hop(i, j, o, x_first):
        at = lax.rem((cy if x_first else cx) + o, R)
        to = along_y(o) if x_first else along_x(o)
        s = sm[f"two{i}{j}"]
        return remote(r[f"two{i}{j}"].at[at], r[f"gat{i}{j}"].at[o - 1], s.at[0, o], s.at[1, o], to)

    def start_first(i):
        for j, (_, _, x_first) in enumerate(p.parts[i]):
            for o in range(1, R):
                first_hop(i, j, o, x_first).start()

    def start_second(i):
        for j, (_, cols, x_first) in enumerate(p.parts[i]):
            t = r[f"one{i}{j}"][cx if x_first else cy].astype(F32)
            for o in range(1, R):
                first_hop(i, j, o, x_first).wait_recv()
                t = t + r[f"got{i}{j}"][o - 1].astype(F32)
            r[f"two{i}{j}"][...] = t.astype(BF).reshape(R, p.own, cols)
            for o in range(1, R):
                second_hop(i, j, o, x_first).start()

    def z_hop(i, o):
        to = lax.rem(z + o, Z)
        s = sm[f"zr{i}"]
        return remote(r[f"zs{i}"].at[to], r[f"zr{i}"].at[o], s.at[0, o], s.at[1, o], me, to)

    def z_gather(i, o):
        to = lax.rem(z + o, Z)
        s = sm[f"zo{i}"]
        return remote(r[f"zo{i}"].at[z], r[f"zo{i}"].at[z], s.at[0, o], s.at[1, o], me, to)

    def loop_z(f):
        def body(o, c):
            f(o)
            return c

        lax.fori_loop(1, Z, body, 0)

    def tiles_of(i):
        per_z = r[f"zs{i}"].shape[1] // 8
        ncb = sum(c for _, c, _ in p.parts[i]) // HEAD
        for t in range(per_z * Z):
            yield t // per_z, (t % per_z) * 8, (t // ncb) * 8, (t % ncb) * HEAD

    def start_z(i):
        pieces = []
        for j, (_, _, x_first) in enumerate(p.parts[i]):
            t = r[f"two{i}{j}"][cy if x_first else cx].astype(F32)
            for o in range(1, R):
                second_hop(i, j, o, x_first).wait_recv()
                t = t + r[f"gat{i}{j}"][o - 1].astype(F32)
            pieces.append(t)
        width = pieces[0].shape[1]
        for zi, zr, ro, co in tiles_of(i):
            part = pieces[co // width]
            co = co % width
            r[f"zs{i}"][zi, zr : zr + 8] = part[ro : ro + 8, co : co + HEAD]
        loop_z(lambda o: z_hop(i, o).start())

    def start_gather(i):
        loop_z(lambda o: z_hop(i, o).wait_recv())
        t = r[f"zs{i}"][z]
        for o in range(1, Z):
            t = t + r[f"zr{i}"][o]
        r[f"zo{i}"][z] = t * ((Z * N * rows) ** -0.5)
        loop_z(lambda o: z_gather(i, o).start())

    def finish(i):
        loop_z(lambda o: z_gather(i, o).wait_recv())
        for zi, zr, ro, co in tiles_of(i):
            val = r[f"zo{i}"][zi, zr : zr + 8]
            if i == 0:
                gq_ref[ro : ro + 8, co : co + HEAD] = val
            elif co < p.kv_cols:
                gk_ref[ro : ro + 8, co : co + HEAD] = val
            else:
                gv_ref[ro : ro + 8, co - p.kv_cols : co - p.kv_cols + HEAD] = val

    pass2(0)
    ret4(0)
    pass2(1)
    dq_copy = remote(r["dq"], r["dqp"], sm["dq"].at[0], sm["dq"].at[1], peer)
    dq_copy.start()
    ret4(1)
    ret2(0)
    tokt_copy.wait_recv()
    dq_copy.wait_recv()
    half = p.q_cols // 2
    made(0, lambda j: (lambda: r["dq"][:, j * half : (j + 1) * half], lambda: r["dqp"][:, j * half : (j + 1) * half]))
    start_first(0)
    ret2(1)

    def gi_q(n, c):
        at = pl.ds(pl.multiple_of(n * step, step), step)
        r["gi32"][:, at] = nt(r["dq"][...], r["wq"][at])
        return c

    lax.fori_loop(0, p.width // step, gi_q, 0)
    ret0(0)
    ret0(1)
    dkv_copy = remote(r["dkv"], r["dkvp"], sm["dkv"].at[0], sm["dkv"].at[1], peer)
    dkv_copy.start()

    def gi_kv(n, c):
        at = pl.ds(pl.multiple_of(n * step, step), step)
        val = r["gi32"][:, at] + nt(r["dkv"][0], r["wk"][at]) + nt(r["dkv"][1], r["wv"][at])
        r["gi"][:, at] = val.astype(BF)
        return c

    lax.fori_loop(0, p.width // step, gi_kv, 0)
    out_copy = pltpu.make_async_copy(r["gi"], gi_h, sm["out"])
    out_copy.start()
    dkv_copy.wait_recv()
    made(1, lambda j: (lambda: r["dkv"][j], lambda: r["dkvp"][j]))
    start_first(1)
    start_second(0)
    start_second(1)
    start_z(0)
    start_z(1)
    start_gather(0)
    start_gather(1)
    finish(0)
    finish(1)

    out_copy.wait()
    for k, (src, dst, to) in enumerate(((0, 2, nxt), (0, 1, peer), (2, 4, nxt), (2, 3, peer))):
        halo(k, src, dst, to).wait_send()
    tokt_copy.wait_send()
    dq_copy.wait_send()
    dkv_copy.wait_send()
    for g in range(p.groups):
        for d, to in ((3, peer), (1, peer), (4, prv), (2, prv)):
            ret(g, d, to).wait_send()
    for i in range(2):
        for j, (_, _, x_first) in enumerate(p.parts[i]):
            for o in range(1, R):
                first_hop(i, j, o, x_first).wait_send()
                second_hop(i, j, o, x_first).wait_send()
        loop_z(lambda o: z_hop(i, o).wait_send())
        loop_z(lambda o: z_gather(i, o).wait_send())


def body(sizes, tokens, w_query, key_weight, value_weight, cotangent, segment_ids):
    rows, width = tokens.shape[1:]
    q_cols, kv_cols = w_query.shape[1], key_weight.shape[1]
    p = build_plan(sizes, rows, width, q_cols, kv_cols, segment_ids.shape[1])
    anyspace = pl.BlockSpec(memory_space=pl.ANY)
    vmem = pl.BlockSpec(memory_space=pltpu.VMEM)
    out = pl.pallas_call(
        functools.partial(kernel, p),
        out_shape=(
            jax.ShapeDtypeStruct((rows, width), BF),
            jax.ShapeDtypeStruct((p.own, q_cols), F32),
            jax.ShapeDtypeStruct((p.own, kv_cols), F32),
            jax.ShapeDtypeStruct((p.own, kv_cols), F32),
        ),
        in_specs=[anyspace] * 6,
        out_specs=(anyspace, vmem, vmem, vmem),
        scratch_shapes=list(p.scratch.values()) + list(p.sems.values()),
        compiler_params=pltpu.CompilerParams(
            collective_id=0, has_side_effects=True, vmem_limit_bytes=60 * 1024 * 1024
        ),
        name="step",
    )(tokens[0], w_query, key_weight, value_weight, cotangent[0], segment_ids)
    return out[0][None], out[1], out[2], out[3]


def solution(mesh):
    sizes = dict(mesh.shape)
    placed = (P("dp", "ctx", None), P(), P(), P(), P("dp", "ctx", None), P("dp", None))
    return jax.shard_map(
        functools.partial(body, sizes),
        mesh=mesh,
        in_specs=placed,
        out_specs=(P("dp", "ctx", None), P("ctx", None), P("ctx", None), P("ctx", None)),
        check_vma=False,
    )
```

time: 434 us -> 105 us (0.24)
  waiting for transfers between devices: 140 us -> 0 us
  Pallas kernels: 0 us -> 97.7 us
  matrix products: 86.7 us -> 0 us
  blocking collectives: 66 us -> 0 us
  starting transfers between devices: 41.1 us -> 0 us
  local copies, waits for them, and re-layouts: 42.5 us -> 6.18 us
  loops' own time: 26.3 us -> 0 us
  between operations: 14.5 us -> 0.64 us
  other arithmetic: 13.1 us -> 0 us
    unnamed x2 -> x0, waiting for transfers between devices: 109 us -> none
    pallas_call x0 -> x1, Pallas kernels: none -> 97.7 us  [body(): pl.pallas_call(functools.partial(kernel, p), out_shape=(jax.ShapeDtypeStr...]
    dot_general x55 -> x0, matrix products: 86.7 us -> none  [the longest x8 17.7 us: head_terms(): jnp.dot(weights_b.T, dout, preferred_element_type=jnp.float32)]
    psum x1 -> x0, blocking collectives: 66 us -> none  [body(): summed = lax.psum(summed, 'dp')]
    ppermute x16 -> x0, starting transfers between devices: 41.1 us -> none  [shifted(): return lax.ppermute(block, axis, route)]
    ppermute x16 -> x0, waiting for transfers between devices: 31 us -> none  [shifted(): return lax.ppermute(block, axis, route)]
    another operation x1 -> x0, loops' own time: 26.3 us -> none  [body(): lax.map(lambda head_index: head_terms(head_index, queries, k_block, v_blo...]
    slice x14 -> x0, local copies, waits for them, and re-layouts: 13.6 us -> none  [the longest x12 13.5 us: piece(): return (dk_local[first:first + rows], dv_local[first:first + rows])]
  transfers between devices with their start and end apart: 17 -> 0, of which waited for: 7 -> 0; matrix products, arithmetic and copies ran while one was open for 6% -> 0% of each run, Pallas kernels for 0% -> 0%
where the time goes in v1:
time: 105 us
  Pallas kernels  97.7 us (93%)
  local copies, waits for them, and re-layouts  6.18 us (6%)
    pallas_call x1, Pallas kernels, body(): pl.pallas_call(functools.partial(kernel, p), out_shape=(jax.ShapeDtypeStr...  97.7 us
    unnamed x4, local copies, waits for them, and re-layouts  6.18 us

profile of v1, /device:TPU:24, one launch (start us, length us, event | category | flops | bytes accessed | tf_op | source)
XLA Modules:
  0.0 104.5 jit_solution(16010379836522684722)
XLA Ops:
  0.6 97.7 %step.1 = (bf16[256,1024]{1,0:T(8,128)(2,1)}, f32[32,1024]{1,0:T(8,128)}, f32[32,256]{1,0:T(8,128)}, f32[32,256]{1,0:T(8,128)}) custom-call(bf16[256,1024]{1,0:T(8,128)(2,1)} %bitcast.4, bf16[1024,1024]{1,0:T(8,128)(2,1)} %wq_h.1, bf16[1024,256]{1,0:T(8,128)(2,1)} %wk_h.1, bf16[1024,256]{1,0:T(8,128)(2,1)} %wv_h.1, bf16[256,1024]{1,0:T(8,128)(2,1)} %bitcast.5, ...), custom_call_target="tpu_custom_call" | custom-call | tf_op jit(solution)/shard_map/step/pallas_call | solution.py:500
  98.3 1.9 %copy.14 = bf16[1,256,1024]{2,1,0:T(8,128)(2,1)} copy(bf16[1,256,1024]{2,1,0:T(8,128)(2,1)} %bitcast.3) | data formatting | bytes 1048576
  100.2 1.6 %copy.15 = f32[32,1024]{1,0:T(8,128)} copy(f32[32,1024]{1,0:T(8,128)} %get-tuple-element.17) | data formatting | bytes 262144
  101.8 1.4 %copy.16 = f32[32,256]{1,0:T(8,128)} copy(f32[32,256]{1,0:T(8,128)} %get-tuple-element.18) | data formatting | bytes 65536
  103.1 1.4 %copy.17 = f32[32,256]{1,0:T(8,128)} copy(f32[32,256]{1,0:T(8,128)} %get-tuple-element.19) | data formatting | bytes 65536

commit v2 on v1

v2 whole, which is shorter than its diff:
```python
import functools
import math

import jax
import jax.numpy as jnp
from jax import lax
from jax.experimental import pallas as pl
from jax.experimental.pallas import tpu as pltpu
from jax.sharding import PartitionSpec as P

HEAD = 128
WINDOW = 1024
NEG = -1e30
VMEM_LIMIT = 54 * 1024 * 1024
BF = jnp.bfloat16
F32 = jnp.float32
MESH = pl.DeviceIdType.MESH
TRACE = False


def mark(name, f, *a):
    if not TRACE:
        return f(*a)
    with jax.named_scope(name):
        return f(*a)


def nn(a, b):
    return lax.dot_general(a, b, (((1,), (0,)), ((), ())), preferred_element_type=F32)


def nt(a, b):
    return lax.dot_general(a, b, (((1,), (1,)), ((), ())), preferred_element_type=F32)


def tn(a, b):
    return lax.dot_general(a, b, (((0,), (0,)), ((), ())), preferred_element_type=F32)


class Plan:
    def __init__(self, sizes, rows, width, q_cols, kv_cols, length):
        self.Z, self.N = sizes["dp"], sizes["ctx"]
        self.X = self.Y = math.isqrt(self.N // 2)
        self.rows, self.width, self.q_cols, self.kv_cols = rows, width, q_cols, kv_cols
        self.length = length
        self.heads = q_cols // HEAD
        self.groups = kv_cols // HEAD
        self.per = self.heads // self.groups
        self.reach = WINDOW // rows
        self.chips = self.N // 2
        self.own = width // self.N
        half = q_cols // 2
        self.q_pieces = ((0, half, True), (half, half, True))
        self.kv_pieces = ((q_cols, kv_cols, True), (q_cols + kv_cols, kv_cols, False))
        self.parts = (self.q_pieces, self.kv_pieces)
        self.scratch = {}
        self.sems = {}

    def cut(self, phase, part):
        if phase == "one":
            return 0 if part == 0 else self.X * self.own // 2
        return self.own // 2

    def buf(self, name, shape, dtype):
        self.scratch[name] = pltpu.VMEM(shape, dtype)

    def sem(self, name, *shape):
        self.sems[name] = pltpu.SemaphoreType.DMA(shape)


def build_plan(sizes, rows, width, q_cols, kv_cols, length):
    p = Plan(sizes, rows, width, q_cols, kv_cols, length)
    lanes = p.per * rows
    blocks = p.reach + 1
    p.buf("tok", (rows, width), BF)
    p.buf("wq", (width, q_cols), BF)
    p.buf("wk", (width, kv_cols), BF)
    p.buf("wv", (width, kv_cols), BF)
    p.buf("cot", (rows, q_cols), BF)
    p.buf("seg", (1, length), jnp.int32)
    p.buf("kvb", (blocks, 2 * p.groups, rows, HEAD), BF)
    p.buf("qst", (p.groups, lanes, HEAD), BF)
    p.buf("dost", (p.groups, lanes, HEAD), BF)
    p.buf("bias", (blocks, rows, rows), F32)
    p.buf("s", (p.groups, blocks, rows, lanes), F32)
    p.buf("dp", (p.groups, blocks, rows, lanes), F32)
    p.buf("relay", (2, rows, HEAD), BF)
    p.buf("m", (p.groups, 8, lanes), F32)
    p.buf("top", (p.groups, 8, lanes), F32)
    p.buf("l", (p.groups, 8, lanes), F32)
    p.buf("de", (p.groups, 8, lanes), F32)
    p.buf("fac", (p.groups, 8, lanes), F32)
    p.buf("acc", (p.groups, blocks, 2, rows, HEAD), F32)
    p.buf("dqt", (p.groups, HEAD, lanes), F32)
    p.buf("relay_back", (p.groups, rows, HEAD), BF)
    p.buf("far", (p.groups, rows, HEAD), BF)
    p.buf("stage", (p.groups, blocks, 2, rows, HEAD), BF)
    p.buf("back", (p.groups, blocks, 2, rows, HEAD), BF)
    p.buf("tokt", (2, width // 2, rows), BF)
    p.buf("toktp", (width // 2, rows), BF)
    p.buf("dq", (rows, q_cols), BF)
    p.buf("dqp", (rows, q_cols), BF)
    p.buf("dkv", (p.groups, 2, rows, HEAD), BF)
    p.buf("dkvp", (p.groups, 2, rows, HEAD), BF)
    p.buf("gi32", (rows, width), F32)
    own, R = p.own, p.X
    for i, part in enumerate(p.parts):
        for j, (first, cols, x_first) in enumerate(part):
            for k, n in (("one", R * own), ("two", own)):
                cut = p.cut(k, i)
                name = f"{k}{i}{j}"
                p.buf(name, (R, n, cols), BF)
                if cut:
                    p.buf(name + "down", (cut, cols), BF)
                p.buf(name + "up", (n - cut, cols), BF)
                p.buf(name + "left", (n, cols), BF)
                p.buf(name + "right", (n, cols), BF)
                p.sem(name, 2, 6)
        tiles = own // 8 * sum(c for _, c, _ in part) // HEAD
        p.buf(f"zs{i}", (p.Z, tiles // p.Z * 8, HEAD), F32)
        p.buf(f"zr{i}", (p.Z, tiles // p.Z * 8, HEAD), F32)
        p.buf(f"zo{i}", (p.Z, tiles // p.Z * 8, HEAD), F32)
        p.sem(f"zr{i}", 2, p.Z)
        p.sem(f"zo{i}", 2, p.Z)
    p.sem("load", 6)
    p.sems["z_in"] = pltpu.SemaphoreType.REGULAR((2,))
    p.sem("ha", 2, 2 * p.groups)
    p.sem("hb", 2)
    p.sem("hc", 2, p.groups)
    p.sem("hd", 2)
    p.sem("he", 2)
    p.sem("hf", 2)
    p.sem("tokt", 2)
    p.sem("dq", 2)
    p.sem("dkv", 2, p.groups)
    p.sem("far", 2, p.groups)
    p.sem("relay_back", 2, p.groups)
    p.sem("ret", 2, p.groups, blocks)
    return p


def kernel(p, tok_h, wq_h, wk_h, wv_h, cot_h, seg_h, gi_ref, gq_ref, gk_ref, gv_ref, *refs):
    names = list(p.scratch)
    r = dict(zip(names, refs[: len(names)]))
    sm = dict(zip(p.sems, refs[len(names) :]))
    rows, lanes, blocks = p.rows, p.per * p.rows, p.reach + 1
    X, Y, Z, N, R = p.X, p.Y, p.Z, p.N, p.X
    z, me = lax.axis_index("dp"), lax.axis_index("ctx")
    core, chip = lax.rem(me, 2), me // 2
    cx, cy = chip // Y, lax.rem(chip, Y)
    peer = me + 1 - 2 * core
    nxt, prv = lax.rem(me + 2, N), lax.rem(me + N - 2, N)
    far_to = lax.rem(cx * Y + lax.rem(cy + 1, Y) + 2, p.chips) * 2 + core
    back2 = lax.rem(chip + p.chips - 2, p.chips)
    far_from = (back2 // Y * Y + lax.rem(lax.rem(back2, Y) + Y - 1, Y)) * 2 + core
    scale = HEAD**-0.5

    def along_x(o):
        return (lax.rem(cx + o, X) * Y + cy) * 2 + core

    def along_y(o):
        return (cx * Y + lax.rem(cy + o, Y)) * 2 + core

    def remote(src, dst, send, recv, ctx, dp=None):
        return pltpu.make_async_remote_copy(
            src_ref=src, dst_ref=dst, send_sem=send, recv_sem=recv,
            device_id=(z if dp is None else dp, ctx), device_id_type=MESH,
        )

    loads = {}
    for i, (name, src) in enumerate(
        (("tok", tok_h), ("wk", wk_h), ("wv", wv_h), ("wq", wq_h), ("cot", cot_h), ("seg", seg_h))
    ):
        loads[name] = pltpu.make_async_copy(src, r[name], sm["load"].at[i])
        loads[name].start()
    barrier = pltpu.get_barrier_semaphore()

    def greet(ctx, dp):
        pl.semaphore_signal(barrier, inc=1, device_id=(dp, ctx), device_id_type=MESH)

    near_z = min(3, Z)
    for o in range(1, near_z):
        greet(me, lax.rem(z + o, Z))
        greet(me, lax.rem(z + Z - o, Z))
    ring = [along_x(o) for o in (1, X - 1)] + [along_y(o) for o in (1, Y - 1)]
    for d in [peer, nxt, prv, far_to, far_from] + ring:
        greet(d, z)

    def z_round(k, distance):
        if Z <= distance:
            return
        for to in (lax.rem(z + distance, Z), lax.rem(z + Z - distance, Z)):
            pl.semaphore_signal(sm["z_in"].at[k], inc=1, device_id=(to, me), device_id_type=MESH)

    def z_joined(k, distance):
        if Z > distance:
            pl.semaphore_wait(sm["z_in"].at[k], 2)

    mark("w_tok", lambda: [loads[name].wait() for name in ("tok", "wk", "wv")])
    for i, w in enumerate(("wk", "wv")):
        val = nn(r["tok"][...], r[w][...]).astype(BF)
        for g in range(p.groups):
            r["kvb"][0, i * p.groups + g] = val[:, g * HEAD : (g + 1) * HEAD]
    mark('w_bar', pl.semaphore_wait, barrier, 9 + 2 * (near_z - 1))
    z_round(0, 2)

    kvb = r["kvb"]

    G, both = p.groups, 2 * p.groups
    up = along_y(Y - 1)

    def pair(name, *at):
        x = sm[name]
        return x.at[(0, *at)], x.at[(1, *at)]

    def h_next(u):
        return remote(kvb.at[0, u], kvb.at[2, u], *pair("ha", u), nxt)

    def h_one(src):
        return remote(kvb.at[src], kvb.at[1], *pair("hb"), peer)

    def h_four(u):
        return remote(kvb.at[2, u], kvb.at[4, u], *pair("hc", u), nxt)

    def h_three(src):
        return remote(kvb.at[src], kvb.at[3], *pair("hd"), peer)

    far_one = remote(kvb.at[0, pl.ds(G, G)], r["relay"], *pair("he"), up)
    far_two = remote(r["relay"], kvb.at[4, pl.ds(G, G)], *pair("hf"), far_to)
    h_next(0).start()
    far_one.start()
    for u in range(1, both):
        h_next(u).start()

    @pl.when(core == 0)
    def _():
        h_one(0).start()

    mark("w_wq", loads["wq"].wait)
    step = 2 * HEAD
    for n in range(p.q_cols // step):
        val = nn(r["tok"][...], r["wq"][:, n * step : (n + 1) * step]).astype(BF)
        for j in range(2):
            g, h = divmod(2 * n + j, p.per)
            r["qst"][g, h * rows : (h + 1) * rows] = val[:, j * HEAD : (j + 1) * HEAD]
    mark("w_cot", loads["cot"].wait)
    for n in range(p.heads):
        g, h = divmod(n, p.per)
        r["dost"][g, h * rows : (h + 1) * rows] = r["cot"][:, n * HEAD : (n + 1) * HEAD]

    mark("w_seg", loads["seg"].wait)
    start = me * rows
    seg = r["seg"][...]
    q_seg = r["seg"][:, pl.ds(pl.multiple_of(start, rows), rows)]
    doc = jnp.zeros((1, rows), jnp.int32)
    for t in range(1, 4):
        below = jnp.sum((seg < t).astype(F32), axis=1, keepdims=True)
        doc = jnp.where(q_seg >= t, below.astype(jnp.int32), doc)
    row = lax.broadcasted_iota(jnp.int32, (rows, rows), 0)
    col = lax.broadcasted_iota(jnp.int32, (rows, rows), 1)
    for b in range(blocks):
        j = row + (start - b * rows)
        gap = col - row + b * rows
        ok = (j >= doc) & (gap >= 0) & (gap < WINDOW)
        r["bias"][b] = jnp.where(ok, 0.0, NEG)

    for n in range(p.width // HEAD):
        val = r["tok"][:, n * HEAD : (n + 1) * HEAD].astype(F32).T.astype(BF)
        for k in range(HEAD // p.own):
            ch, c = divmod(n * (HEAD // p.own) + k, 2)
            r["tokt"][c, ch * p.own : (ch + 1) * p.own] = val[k * p.own : (k + 1) * p.own]
    tokt_copy = remote(r["tokt"].at[1 - core], r["toktp"], sm["tokt"].at[0], sm["tokt"].at[1], peer)
    tokt_copy.start()

    r["m"][...] = jnp.full(r["m"].shape, -3e38, F32)

    def pass1(b):
        def body(g, c):
            kk, vv = kvb[b, g], kvb[b, p.groups + g]
            for h in range(p.per):
                cols = slice(h * rows, (h + 1) * rows)
                s = nt(kk, r["qst"][g, cols]) + r["bias"][b]
                r["s"][g, b, :, cols] = s
                r["m"][g, :, cols] = jnp.maximum(
                    r["m"][g, :, cols], jnp.max(s.reshape(rows // 8, 8, rows), axis=0)
                )
                r["dp"][g, b, :, cols] = nt(vv, r["dost"][g, cols])
            return c

        lax.fori_loop(0, p.groups, body, 0)

    mark("pass1_0", pass1, 0)
    for u in range(G):
        mark("w_next", h_next(u).wait_recv)
        h_four(u).start()
    mark("w_far", far_one.wait_recv)
    far_two.start()
    for u in range(G, both):
        mark("w_next2", h_next(u).wait_recv)

    @pl.when(core == 0)
    def _():
        h_three(2).start()

    @pl.when(core == 1)
    def _():
        h_one(2).start()

    mark("pass1_2", pass1, 2)
    mark("w_one", h_one(0).wait_recv)
    mark("pass1_1", pass1, 1)

    r["l"][...] = jnp.zeros(r["l"].shape, F32)
    r["de"][...] = jnp.zeros(r["de"].shape, F32)

    def expo(g, b):
        for h in range(p.per):
            cols = slice(h * rows, (h + 1) * rows)
            e = jnp.exp((r["s"][g, b, :, cols] - r["top"][g, 0:1, cols]) * scale)
            r["s"][g, b, :, cols] = e
            r["l"][g, :, cols] += jnp.sum(e.reshape(rows // 8, 8, rows), axis=0)
            de = e * r["dp"][g, b, :, cols]
            r["de"][g, :, cols] += jnp.sum(de.reshape(rows // 8, 8, rows), axis=0)

    def early(g, c):
        r["top"][g] = jnp.broadcast_to(jnp.max(r["m"][g], axis=0, keepdims=True), (8, lanes))

        def one(b, c2):
            expo(g, b)
            return c2

        return lax.fori_loop(0, 3, one, c)

    def late(g, c):
        top = jnp.broadcast_to(jnp.max(r["m"][g], axis=0, keepdims=True), (8, lanes))
        down = jnp.exp((r["top"][g] - top) * scale)
        r["top"][g] = top
        r["fac"][g] = down
        r["l"][g] *= down
        r["de"][g] *= down

        def one(b, c2):
            expo(g, b)
            return c2

        lax.fori_loop(3, blocks, one, c)
        inv = 1.0 / jnp.sum(r["l"][g], axis=0, keepdims=True)
        delta = jnp.sum(r["de"][g], axis=0, keepdims=True) * inv
        r["l"][g] = jnp.broadcast_to(inv, (8, lanes))
        r["de"][g] = jnp.broadcast_to(delta, (8, lanes))
        return c

    z_joined(0, 2)
    z_round(1, 4)
    mark("early", lax.fori_loop, 0, G, early, 0)
    for u in range(G):
        mark("w_four", h_four(u).wait_recv)
    mark("w_far2", far_two.wait_recv)

    @pl.when(core == 1)
    def _():
        h_three(4).start()

    mark("pass1_4", pass1, 4)
    mark("w_three", h_three(2).wait_recv)
    mark("pass1_3", pass1, 3)
    mark("late", lax.fori_loop, 0, G, late, 0)

    acc, stage, back = r["acc"], r["stage"], r["back"]
    first_core = (core == 0).astype(F32)
    second_core = (core == 1).astype(F32)
    r["dqt"][...] = jnp.zeros(r["dqt"].shape, F32)

    def grads(b):
        def body(g, c):
            kk = kvb[b, g]
            dv = jnp.zeros((rows, HEAD), F32)
            dk = jnp.zeros((rows, HEAD), F32)
            for h in range(p.per):
                cols = slice(h * rows, (h + 1) * rows)
                inv = r["l"][g, 0:1, cols]
                if b < 3:
                    inv = inv * r["fac"][g, 0:1, cols]
                prob = r["s"][g, b, :, cols] * inv
                ds = (prob * (r["dp"][g, b, :, cols] - r["de"][g, 0:1, cols]) * scale).astype(BF)
                dv = dv + nn(prob.astype(BF), r["dost"][g, cols])
                dk = dk + nn(ds, r["qst"][g, cols])
                r["dqt"][g, :, cols] += tn(kk, ds)
            acc[g, b, 0] = dk
            acc[g, b, 1] = dv
            if b in (1, 3, 4):
                stage[g, b, 0] = dk.astype(BF)
                stage[g, b, 1] = dv.astype(BF)
            return c

        lax.fori_loop(0, G, body, 0)

    def ret(g, d, to):
        return remote(stage.at[g, d], back.at[g, d], *pair("ret", g, d), to)

    def ret_four(g):
        return remote(stage.at[g, 4, 0], back.at[g, 4, 0], *pair("ret", g, 4), prv)

    def far_send(g):
        return remote(stage.at[g, 4, 1], r["relay_back"].at[g], *pair("relay_back", g), far_from)

    def far_last(g):
        return remote(r["relay_back"].at[g], r["far"].at[g], *pair("far", g), along_y(1))

    def to_peer(d):
        for g in range(G):
            ret(g, d, peer).start()

    def ret4(g):
        @pl.when(core == 1)
        def _():
            ret(g, 3, peer).wait_recv()
            stage[g, 4] = (acc[g, 4] + back[g, 3].astype(F32)).astype(BF)

        ret_four(g).start()
        far_send(g).start()

    def forward_far(g):
        far_send(g).wait_recv()
        far_last(g).start()

    def ret2(g):
        @pl.when(core == 0)
        def _():
            ret(g, 3, peer).wait_recv()

        ret(g, 1, peer).wait_recv()
        ret_four(g).wait_recv()
        t = acc[g, 2] + first_core * back[g, 3].astype(F32) + second_core * back[g, 1].astype(F32)
        stage[g, 2, 0] = (t[0] + back[g, 4, 0].astype(F32)).astype(BF)
        stage[g, 2, 1] = t[1].astype(BF)
        ret(g, 2, prv).start()

    def dkv_copy(g):
        return remote(r["dkv"].at[g], r["dkvp"].at[g], *pair("dkv", g), peer)

    def ret0(g):
        ret(g, 2, prv).wait_recv()
        far_last(g).wait_recv()
        t = acc[g, 0] + back[g, 2].astype(F32) + first_core * back[g, 1].astype(F32)
        r["dkv"][g, 0] = t[0].astype(BF)
        r["dkv"][g, 1] = (t[1] + r["far"][g].astype(F32)).astype(BF)
        dkv_copy(g).start()

    def made(one, x_first, at, mine, other):
        val = (nn(r["tokt"][core], mine) + nn(r["toktp"][...], other)).astype(BF)
        if x_first:
            one[:, :, at] = val.reshape(X, Y * p.own, val.shape[1])
        else:
            for a in range(X):
                for k in range(Y):
                    ro = (a * Y + k) * p.own
                    one[k, a * p.own : (a + 1) * p.own, at] = val[ro : ro + p.own]

    def made_q(j):
        first, cols, x_first = p.parts[0][j]

        def body(n, c):
            to = pl.ds(pl.multiple_of(n * step, step), step)
            at = pl.ds(pl.multiple_of(first + n * step, step), step)
            made(r[f"one0{j}"], x_first, to, r["dq"][:, at], r["dqp"][:, at])
            return c

        lax.fori_loop(0, cols // step, body, 0)

    def made_kv(j):
        def wide(name):
            return jnp.concatenate([r[name][g, j] for g in range(G)], axis=1)

        made(r[f"one1{j}"], p.parts[1][j][2], slice(0, p.kv_cols), wide("dkv"), wide("dkvp"))

    class Ring:
        def __init__(self, k, i, j):
            x_first = p.parts[i][j][2]
            on_x = x_first == (k == "one")
            self.name, self.cut = f"{k}{i}{j}", p.cut(k, i)
            self.at, along = (cx, along_x) if on_x else (cy, along_y)
            self.next, self.prev = along(1), along(R - 1)
            self.n = r[self.name].shape[1]

        def chunk(self, o):
            return r[self.name].at[lax.rem(self.at + o, R)]

        def copy(self, k, src, dst, to):
            return remote(src, dst, *pair(self.name, k), to)

        def two_up(self):
            return self.copy(0, self.chunk(2).at[self.cut :], r[self.name + "up"], self.next)

        def two_down(self):
            return self.copy(1, self.chunk(2).at[: self.cut], r[self.name + "down"], self.prev)

        def up(self, rows, k):
            return self.copy(k, self.chunk(1).at[rows], r[self.name + "left"].at[rows], self.next)

        def down(self, rows, k):
            return self.copy(k, self.chunk(R - 1).at[rows], r[self.name + "right"].at[rows], self.prev)

        def start_up(self):
            self.two_up().start()
            if self.cut:
                self.up(slice(0, self.cut), 2).start()

        def start_down(self):
            if self.cut:
                self.two_down().start()
            self.down(slice(self.cut, self.n), 3).start()

        def add(self, o, rows, name):
            k = lax.rem(self.at + o, R)
            val = r[self.name][k, rows].astype(F32) + r[self.name + name][...].astype(F32)
            r[self.name][k, rows] = val.astype(BF)

        def pass_up(self):
            self.two_up().wait_recv()
            self.add(1, slice(self.cut, self.n), "up")
            self.up(slice(self.cut, self.n), 4).start()

        def pass_down(self):
            if self.cut:
                self.two_down().wait_recv()
                self.add(R - 1, slice(0, self.cut), "down")
                self.down(slice(0, self.cut), 5).start()

        def copies(self, whole=True):
            if whole:
                yield self.two_up()
            yield self.down(slice(self.cut, self.n), 3)
            yield self.up(slice(self.cut, self.n), 4)
            if self.cut:
                if whole:
                    yield self.two_down()
                yield self.up(slice(0, self.cut), 2)
                yield self.down(slice(0, self.cut), 5)

        def total(self):
            for copy in self.copies(whole=False):
                copy.wait_recv()
            t = r[self.name][self.at].astype(F32)
            return t + r[self.name + "left"][...].astype(F32) + r[self.name + "right"][...].astype(F32)

    one = [[Ring("one", i, j) for j in range(2)] for i in range(2)]
    two = [[Ring("two", i, j) for j in range(2)] for i in range(2)]

    def start_second(i):
        for j in range(2):
            t = one[i][j].total().astype(BF)
            r[f"two{i}{j}"][...] = t.reshape(R, p.own, t.shape[1])
            two[i][j].start_up()
            two[i][j].start_down()

    def pass_second(i):
        for j in range(2):
            two[i][j].pass_up()
            two[i][j].pass_down()

    def z_hop(i, o):
        to = lax.rem(z + o, Z)
        s = sm[f"zr{i}"]
        return remote(r[f"zs{i}"].at[to], r[f"zr{i}"].at[o], s.at[0, o], s.at[1, o], me, to)

    def z_gather(i, o):
        to = lax.rem(z + o, Z)
        s = sm[f"zo{i}"]
        return remote(r[f"zo{i}"].at[z], r[f"zo{i}"].at[z], s.at[0, o], s.at[1, o], me, to)

    def loop_z(f):
        def body(o, c):
            f(o)
            return c

        lax.fori_loop(1, Z, body, 0)

    def tiles_of(i):
        per_z = r[f"zs{i}"].shape[1] // 8
        ncb = sum(c for _, c, _ in p.parts[i]) // HEAD
        for t in range(per_z * Z):
            yield t // per_z, (t % per_z) * 8, (t // ncb) * 8, (t % ncb) * HEAD

    def start_z(i):
        pieces = [two[i][j].total() for j in range(2)]
        width = pieces[0].shape[1]
        for zi, zr, ro, co in tiles_of(i):
            part = pieces[co // width]
            co = co % width
            r[f"zs{i}"][zi, zr : zr + 8] = part[ro : ro + 8, co : co + HEAD]
        loop_z(lambda o: z_hop(i, o).start())

    def start_gather(i):
        loop_z(lambda o: z_hop(i, o).wait_recv())
        t = r[f"zs{i}"][z]
        for o in range(1, Z):
            t = t + r[f"zr{i}"][o]
        r[f"zo{i}"][z] = t * ((Z * N * rows) ** -0.5)
        loop_z(lambda o: z_gather(i, o).start())

    def finish(i):
        loop_z(lambda o: z_gather(i, o).wait_recv())
        for zi, zr, ro, co in tiles_of(i):
            val = r[f"zo{i}"][zi, zr : zr + 8]
            if i == 0:
                gq_ref[ro : ro + 8, co : co + HEAD] = val
            elif co < p.kv_cols:
                gk_ref[ro : ro + 8, co : co + HEAD] = val
            else:
                gv_ref[ro : ro + 8, co - p.kv_cols : co - p.kv_cols + HEAD] = val

    z_joined(1, 4)
    mark("grads3", grads, 3)
    to_peer(3)
    mark("grads1", grads, 1)
    to_peer(1)
    mark("grads4", grads, 4)
    mark("ret4", lambda: [ret4(g) for g in range(G)])
    mark("grads2", grads, 2)
    mark("grads0", grads, 0)

    def dq_rows():
        for n in range(p.heads):
            g, h = divmod(n, p.per)
            r["dq"][:, n * HEAD : (n + 1) * HEAD] = r["dqt"][g, :, h * rows : (h + 1) * rows].T.astype(BF)

    mark("dq_rows", dq_rows)
    dq_copy = remote(r["dq"], r["dqp"], *pair("dq"), peer)
    dq_copy.start()
    mark("w_dq", lambda: (tokt_copy.wait_recv(), dq_copy.wait_recv()))
    mark("made_q", made_q, 0)
    one[0][0].start_up()
    mark("fwd_far", lambda: [forward_far(g) for g in range(G)])
    mark("ret2_0", ret2, 0)
    mark("made_q", made_q, 1)
    one[0][1].start_up()
    mark("ret2_1", ret2, 1)

    def gi_q(n, c):
        at = pl.ds(pl.multiple_of(n * step, step), step)
        r["gi32"][:, at] = nt(r["dq"][...], r["wq"][at])
        return c

    mark("gi_q", lax.fori_loop, 0, p.width // step, gi_q, 0)
    mark("ret0_0", ret0, 0)
    mark("pass_q", one[0][0].pass_up)
    one[0][0].start_down()
    mark("ret0_1", ret0, 1)
    mark("pass_q", one[0][1].pass_up)
    one[0][1].start_down()
    mark("w_dkv", lambda: [dkv_copy(g).wait_recv() for g in range(G)])
    for j in range(2):
        mark("made_kv", made_kv, j)
        one[1][j].start_up()
        one[1][j].start_down()

    def gi_kv(n, c):
        at = pl.ds(pl.multiple_of(n * step, step), step)
        val = r["gi32"][:, at]
        for i, w in enumerate(("wk", "wv")):
            for g in range(G):
                val = val + nt(r["dkv"][g, i], r[w][at, g * HEAD : (g + 1) * HEAD])
        gi_ref[:, at] = val.astype(BF)
        return c

    mark("gi_kv", lax.fori_loop, 0, p.width // step, gi_kv, 0)
    mark("pass_kv", lambda: [f() for j in range(2) for f in (one[1][j].pass_up, one[1][j].pass_down)])
    mark("second_0", start_second, 0)
    mark("second_1", start_second, 1)
    mark("pass2_0", pass_second, 0)
    mark("pass2_1", pass_second, 1)
    mark("z_0", start_z, 0)
    mark("z_1", start_z, 1)
    mark("gather_0", start_gather, 0)
    mark("gather_1", start_gather, 1)
    mark("finish_0", finish, 0)
    mark("finish_1", finish, 1)

    for u in range(both):
        h_next(u).wait_send()
    for u in range(G):
        h_four(u).wait_send()
    for copy in (h_one(0), h_three(2), far_one, far_two, tokt_copy, dq_copy):
        copy.wait_send()
    for g in range(G):
        for copy in (ret(g, 3, peer), ret(g, 1, peer), ret(g, 2, prv), ret_four(g), far_send(g), far_last(g), dkv_copy(g)):
            copy.wait_send()
    for i in range(2):
        for ring_sum in one[i] + two[i]:
            for copy in ring_sum.copies():
                copy.wait_send()
        loop_z(lambda o: z_hop(i, o).wait_send())
        loop_z(lambda o: z_gather(i, o).wait_send())


def emit(*refs):
    n = (len(refs) - 1) // 2
    copies = [pltpu.make_async_copy(refs[i], refs[n + i], refs[-1].at[i]) for i in range(n)]
    for c in copies:
        c.start()
    for c in copies:
        c.wait()


def body(sizes, tokens, w_query, key_weight, value_weight, cotangent, segment_ids):
    rows, width = tokens.shape[1:]
    q_cols, kv_cols = w_query.shape[1], key_weight.shape[1]
    p = build_plan(sizes, rows, width, q_cols, kv_cols, segment_ids.shape[1])
    anyspace = pl.BlockSpec(memory_space=pl.ANY)
    vmem = pl.BlockSpec(memory_space=pltpu.VMEM)
    shapes = (
        jax.ShapeDtypeStruct((rows, width), BF),
        jax.ShapeDtypeStruct((p.own, q_cols), F32),
        jax.ShapeDtypeStruct((p.own, kv_cols), F32),
        jax.ShapeDtypeStruct((p.own, kv_cols), F32),
    )
    out = pl.pallas_call(
        functools.partial(kernel, p),
        out_shape=shapes,
        in_specs=[anyspace] * 6,
        out_specs=(vmem,) * 4,
        scratch_shapes=list(p.scratch.values()) + list(p.sems.values()),
        compiler_params=pltpu.CompilerParams(
            collective_id=0, has_side_effects=True, vmem_limit_bytes=VMEM_LIMIT
        ),
        name="step",
    )(tokens[0], w_query, key_weight, value_weight, cotangent[0], segment_ids)
    out = pl.pallas_call(
        emit,
        out_shape=shapes,
        in_specs=[vmem] * 4,
        out_specs=(anyspace,) * 4,
        scratch_shapes=[pltpu.SemaphoreType.DMA((4,))],
        name="emit",
    )(*out)
    return out[0][None], out[1], out[2], out[3]


def solution(mesh):
    sizes = dict(mesh.shape)
    placed = (P("dp", "ctx", None), P(), P(), P(), P("dp", "ctx", None), P("dp", None))
    return jax.shard_map(
        functools.partial(body, sizes),
        mesh=mesh,
        in_specs=placed,
        out_specs=(P("dp", "ctx", None), P("ctx", None), P("ctx", None), P("ctx", None)),
        check_vma=False,
    )
```

time: 105 us -> 86.8 us (0.83)
  Pallas kernels: 97.7 us -> 85.4 us
  local copies, waits for them, and re-layouts: 6.18 us -> 0 us
    pallas_call x1 -> x2, Pallas kernels: 97.7 us -> 85.4 us  [the longest x1 83.4 us: body(): pl.pallas_call(functools.partial(kernel, p), out_shape=shapes, in_specs=[...]
    unnamed x4 -> x0, local copies, waits for them, and re-layouts: 6.18 us -> none
where the time goes in v2:
time: 86.8 us; the launch traced here: 86 us
  Pallas kernels  85.4 us (98%)
    pallas_call x1, Pallas kernels, body(): pl.pallas_call(functools.partial(kernel, p), out_shape=shapes, in_specs=[...  83.4 us
    pallas_call x1, Pallas kernels, body(): pl.pallas_call(emit, out_shape=shapes, in_specs=[vmem] * 4, out_specs=(an...  2 us

profile of v2, /device:TPU:24, one launch (start us, length us, event | category | flops | bytes accessed | tf_op | source)
XLA Modules:
  0.0 86.0 jit_solution(17855893365727741126)
XLA Ops:
  0.6 83.4 %step.1 = (bf16[256,1024]{1,0:T(8,128)(2,1)}, f32[32,1024]{1,0:T(8,128)}, f32[32,256]{1,0:T(8,128)}, f32[32,256]{1,0:T(8,128)}) custom-call(bf16[256,1024]{1,0:T(8,128)(2,1)} %bitcast.3, bf16[1024,1024]{1,0:T(8,128)(2,1)} %wq_h.1, bf16[1024,256]{1,0:T(8,128)(2,1)} %wk_h.1, bf16[1024,256]{1,0:T(8,128)(2,1)} %wv_h.1, bf16[256,1024]{1,0:T(8,128)(2,1)} %bitcast.4, ...), custom_call_target="tpu_custom_call" | custom-call | tf_op jit(solution)/shard_map/step/pallas_call | solution.py:718
  84.0 2.0 %emit.1 = (bf16[256,1024]{1,0:T(8,128)(2,1)}, f32[32,1024]{1,0:T(8,128)}, f32[32,256]{1,0:T(8,128)}, f32[32,256]{1,0:T(8,128)}) custom-call(bf16[256,1024]{1,0:T(8,128)(2,1)} %get-tuple-element.12.refs_0_, f32[32,1024]{1,0:T(8,128)} %get-tuple-element.13.refs_1_, f32[32,256]{1,0:T(8,128)} %get-tuple-element.14.refs_2_, f32[32,256]{1,0:T(8,128)} %get-tuple-element.15.refs_3_), custom_call_target="tpu_custom_call" | custom-call | tf_op jit(solution)/shard_map/emit/pallas_call | solution.py:729

commit v3 on v2

--- a/solution.py
+++ b/solution.py
@@ -55,11 +55,6 @@
         self.parts = (self.q_pieces, self.kv_pieces)
         self.scratch = {}
         self.sems = {}
-
-    def cut(self, phase, part):
-        if phase == "one":
-            return 0 if part == 0 else self.X * self.own // 2
-        return self.own // 2
 
     def buf(self, name, shape, dtype):
         self.scratch[name] = pltpu.VMEM(shape, dtype)
@@ -92,8 +87,8 @@
     p.buf("fac", (p.groups, 8, lanes), F32)
     p.buf("acc", (p.groups, blocks, 2, rows, HEAD), F32)
     p.buf("dqt", (p.groups, HEAD, lanes), F32)
-    p.buf("relay_back", (p.groups, rows, HEAD), BF)
-    p.buf("far", (p.groups, rows, HEAD), BF)
+    p.buf("relay_back", (p.groups, 2, rows, HEAD), BF)
+    p.buf("far", (p.groups, 2, rows, HEAD), BF)
     p.buf("stage", (p.groups, blocks, 2, rows, HEAD), BF)
     p.buf("back", (p.groups, blocks, 2, rows, HEAD), BF)
     p.buf("tokt", (2, width // 2, rows), BF)
@@ -106,20 +101,21 @@
     own, R = p.own, p.X
     for i, part in enumerate(p.parts):
         for j, (first, cols, x_first) in enumerate(part):
-            for k, n in (("one", R * own), ("two", own)):
-                cut = p.cut(k, i)
+            for k, n, kind in (("one", R * own, BF), ("two", own, BF)):
                 name = f"{k}{i}{j}"
-                p.buf(name, (R, n, cols), BF)
-                if cut:
-                    p.buf(name + "down", (cut, cols), BF)
-                p.buf(name + "up", (n - cut, cols), BF)
-                p.buf(name + "left", (n, cols), BF)
-                p.buf(name + "right", (n, cols), BF)
-                p.sem(name, 2, 6)
+                p.buf(name, (R, n, cols), kind)
+                if i or k == "two":
+                    p.buf(name + "got", (R - 1, n, cols), kind)
+                    p.sem(name, 2, R)
+                    continue
+                p.buf(name + "up", (n, cols), kind)
+                p.buf(name + "left", (n, cols), kind)
+                p.buf(name + "right", (n, cols), kind)
+                p.sem(name, 2, 3)
         tiles = own // 8 * sum(c for _, c, _ in part) // HEAD
-        p.buf(f"zs{i}", (p.Z, tiles // p.Z * 8, HEAD), F32)
-        p.buf(f"zr{i}", (p.Z, tiles // p.Z * 8, HEAD), F32)
-        p.buf(f"zo{i}", (p.Z, tiles // p.Z * 8, HEAD), F32)
+        p.buf(f"zs{i}", (p.Z, tiles // p.Z * 8, HEAD), BF)
+        p.buf(f"zr{i}", (p.Z, tiles // p.Z * 8, HEAD), BF)
+        p.buf(f"zo{i}", (p.Z, tiles // p.Z * 8, HEAD), F32 if i else BF)
         p.sem(f"zr{i}", 2, p.Z)
         p.sem(f"zo{i}", 2, p.Z)
     p.sem("load", 6)
@@ -133,8 +129,8 @@
     p.sem("tokt", 2)
     p.sem("dq", 2)
     p.sem("dkv", 2, p.groups)
-    p.sem("far", 2, p.groups)
-    p.sem("relay_back", 2, p.groups)
+    p.sem("far", 2, p.groups, 2)
+    p.sem("relay_back", 2, p.groups, 2)
     p.sem("ret", 2, p.groups, blocks)
     return p
 
@@ -153,6 +149,9 @@
     far_to = lax.rem(cx * Y + lax.rem(cy + 1, Y) + 2, p.chips) * 2 + core
     back2 = lax.rem(chip + p.chips - 2, p.chips)
     far_from = (back2 // Y * Y + lax.rem(lax.rem(back2, Y) + Y - 1, Y)) * 2 + core
+    owner = lax.rem(cx * Y + lax.rem(cy + Y - 1, Y) + p.chips - 2, p.chips) * 2 + core
+    ahead = lax.rem(chip + 2, p.chips)
+    sender = (ahead // Y * Y + lax.rem(lax.rem(ahead, Y) + 1, Y)) * 2 + core
     scale = HEAD**-0.5
 
     def along_x(o):
@@ -183,7 +182,7 @@
         greet(me, lax.rem(z + o, Z))
         greet(me, lax.rem(z + Z - o, Z))
     ring = [along_x(o) for o in (1, X - 1)] + [along_y(o) for o in (1, Y - 1)]
-    for d in [peer, nxt, prv, far_to, far_from] + ring:
+    for d in [peer, nxt, prv, far_to, far_from, owner, sender] + ring:
         greet(d, z)
 
     def z_round(k, distance):
@@ -201,7 +200,7 @@
         val = nn(r["tok"][...], r[w][...]).astype(BF)
         for g in range(p.groups):
             r["kvb"][0, i * p.groups + g] = val[:, g * HEAD : (g + 1) * HEAD]
-    mark('w_bar', pl.semaphore_wait, barrier, 9 + 2 * (near_z - 1))
+    mark('w_bar', pl.semaphore_wait, barrier, 11 + 2 * (near_z - 1))
     z_round(0, 2)
 
     kvb = r["kvb"]
@@ -398,14 +397,15 @@
     def ret(g, d, to):
         return remote(stage.at[g, d], back.at[g, d], *pair("ret", g, d), to)
 
-    def ret_four(g):
-        return remote(stage.at[g, 4, 0], back.at[g, 4, 0], *pair("ret", g, 4), prv)
-
-    def far_send(g):
-        return remote(stage.at[g, 4, 1], r["relay_back"].at[g], *pair("relay_back", g), far_from)
-
-    def far_last(g):
-        return remote(r["relay_back"].at[g], r["far"].at[g], *pair("far", g), along_y(1))
+    units = [(g, i) for g in range(G) for i in range(2)]
+
+    def far_send(g, i):
+        to = prv if (g, i) == (0, 0) else along_y(1)
+        return remote(stage.at[g, 4, i], r["relay_back"].at[g, i], *pair("relay_back", g, i), to)
+
+    def far_last(g, i):
+        to = prv if (g, i) == (0, 0) else owner
+        return remote(r["relay_back"].at[g, i], r["far"].at[g, i], *pair("far", g, i), to)
 
     def to_peer(d):
         for g in range(G):
@@ -417,12 +417,12 @@
             ret(g, 3, peer).wait_recv()
             stage[g, 4] = (acc[g, 4] + back[g, 3].astype(F32)).astype(BF)
 
-        ret_four(g).start()
-        far_send(g).start()
-
-    def forward_far(g):
-        far_send(g).wait_recv()
-        far_last(g).start()
+        for i in range(2):
+            far_send(g, i).start()
+
+    def forward_far(g, i):
+        far_send(g, i).wait_recv()
+        far_last(g, i).start()
 
     def ret2(g):
         @pl.when(core == 0)
@@ -430,10 +430,8 @@
             ret(g, 3, peer).wait_recv()
 
         ret(g, 1, peer).wait_recv()
-        ret_four(g).wait_recv()
         t = acc[g, 2] + first_core * back[g, 3].astype(F32) + second_core * back[g, 1].astype(F32)
-        stage[g, 2, 0] = (t[0] + back[g, 4, 0].astype(F32)).astype(BF)
-        stage[g, 2, 1] = t[1].astype(BF)
+        stage[g, 2] = t.astype(BF)
         ret(g, 2, prv).start()
 
     def dkv_copy(g):
@@ -441,10 +439,10 @@
 
     def ret0(g):
         ret(g, 2, prv).wait_recv()
-        far_last(g).wait_recv()
+        for i in range(2):
+            far_last(g, i).wait_recv()
         t = acc[g, 0] + back[g, 2].astype(F32) + first_core * back[g, 1].astype(F32)
-        r["dkv"][g, 0] = t[0].astype(BF)
-        r["dkv"][g, 1] = (t[1] + r["far"][g].astype(F32)).astype(BF)
+        r["dkv"][g] = (t + r["far"][g].astype(F32)).astype(BF)
         dkv_copy(g).start()
 
     def made(one, x_first, at, mine, other):
@@ -478,10 +476,9 @@
         def __init__(self, k, i, j):
             x_first = p.parts[i][j][2]
             on_x = x_first == (k == "one")
-            self.name, self.cut = f"{k}{i}{j}", p.cut(k, i)
+            self.name = f"{k}{i}{j}"
             self.at, along = (cx, along_x) if on_x else (cy, along_y)
-            self.next, self.prev = along(1), along(R - 1)
-            self.n = r[self.name].shape[1]
+            self.next, self.prev, self.along = along(1), along(R - 1), along
 
         def chunk(self, o):
             return r[self.name].at[lax.rem(self.at + o, R)]
@@ -490,74 +487,56 @@
             return remote(src, dst, *pair(self.name, k), to)
 
         def two_up(self):
-            return self.copy(0, self.chunk(2).at[self.cut :], r[self.name + "up"], self.next)
-
-        def two_down(self):
-            return self.copy(1, self.chunk(2).at[: self.cut], r[self.name + "down"], self.prev)
-
-        def up(self, rows, k):
-            return self.copy(k, self.chunk(1).at[rows], r[self.name + "left"].at[rows], self.next)
-
-        def down(self, rows, k):
-            return self.copy(k, self.chunk(R - 1).at[rows], r[self.name + "right"].at[rows], self.prev)
-
-        def start_up(self):
-            self.two_up().start()
-            if self.cut:
-                self.up(slice(0, self.cut), 2).start()
-
-        def start_down(self):
-            if self.cut:
-                self.two_down().start()
-            self.down(slice(self.cut, self.n), 3).start()
-
-        def add(self, o, rows, name):
-            k = lax.rem(self.at + o, R)
-            val = r[self.name][k, rows].astype(F32) + r[self.name + name][...].astype(F32)
-            r[self.name][k, rows] = val.astype(BF)
+            return self.copy(0, self.chunk(2), r[self.name + "up"], self.next)
+
+        def up(self):
+            return self.copy(1, self.chunk(1), r[self.name + "left"], self.next)
+
+        def down(self):
+            return self.copy(2, self.chunk(R - 1), r[self.name + "right"], self.prev)
 
         def pass_up(self):
             self.two_up().wait_recv()
-            self.add(1, slice(self.cut, self.n), "up")
-            self.up(slice(self.cut, self.n), 4).start()
-
-        def pass_down(self):
-            if self.cut:
-                self.two_down().wait_recv()
-                self.add(R - 1, slice(0, self.cut), "down")
-                self.down(slice(0, self.cut), 5).start()
-
-        def copies(self, whole=True):
-            if whole:
-                yield self.two_up()
-            yield self.down(slice(self.cut, self.n), 3)
-            yield self.up(slice(self.cut, self.n), 4)
-            if self.cut:
-                if whole:
-                    yield self.two_down()
-                yield self.up(slice(0, self.cut), 2)
-                yield self.down(slice(0, self.cut), 5)
+            k = lax.rem(self.at + 1, R)
+            val = r[self.name][k].astype(F32) + r[self.name + "up"][...].astype(F32)
+            r[self.name][k] = val.astype(BF)
+            self.up().start()
+
+        def copies(self):
+            return [self.two_up(), self.up(), self.down()]
 
         def total(self):
-            for copy in self.copies(whole=False):
-                copy.wait_recv()
+            self.up().wait_recv()
+            self.down().wait_recv()
             t = r[self.name][self.at].astype(F32)
             return t + r[self.name + "left"][...].astype(F32) + r[self.name + "right"][...].astype(F32)
 
-    one = [[Ring("one", i, j) for j in range(2)] for i in range(2)]
-    two = [[Ring("two", i, j) for j in range(2)] for i in range(2)]
+    class Direct(Ring):
+        def copies(self):
+            for o in range(1, R):
+                to = self.along(o)
+                yield self.copy(o, self.chunk(o), r[self.name + "got"].at[o - 1], to)
+
+        def start(self):
+            for copy in self.copies():
+                copy.start()
+
+        def total(self):
+            t = r[self.name][self.at].astype(F32)
+            for o, copy in enumerate(self.copies()):
+                copy.wait_recv()
+                t = t + r[self.name + "got"][o].astype(F32)
+            return t
+
+    kinds = (Ring, Direct)
+    one = [[kinds[i]("one", i, j) for j in range(2)] for i in range(2)]
+    two = [[Direct("two", i, j) for j in range(2)] for i in range(2)]
 
     def start_second(i):
         for j in range(2):
-            t = one[i][j].total().astype(BF)
-            r[f"two{i}{j}"][...] = t.reshape(R, p.own, t.shape[1])
-            two[i][j].start_up()
-            two[i][j].start_down()
-
-    def pass_second(i):
-        for j in range(2):
-            two[i][j].pass_up()
-            two[i][j].pass_down()
+            t = one[i][j].total()
+            r[f"two{i}{j}"][...] = t.reshape(R, p.own, t.shape[1]).astype(r[f"two{i}{j}"].dtype)
+            two[i][j].start()
 
     def z_hop(i, o):
         to = lax.rem(z + o, Z)
@@ -570,11 +549,11 @@
         return remote(r[f"zo{i}"].at[z], r[f"zo{i}"].at[z], s.at[0, o], s.at[1, o], me, to)
 
     def loop_z(f):
-        def body(o, c):
-            f(o)
+        def body(k, c):
+            f(Z // 2 + (k + 1) // 2 * (1 - 2 * lax.rem(k, 2)))
             return c
 
-        lax.fori_loop(1, Z, body, 0)
+        lax.fori_loop(0, Z - 1, body, 0)
 
     def tiles_of(i):
         per_z = r[f"zs{i}"].shape[1] // 8
@@ -588,21 +567,21 @@
         for zi, zr, ro, co in tiles_of(i):
             part = pieces[co // width]
             co = co % width
-            r[f"zs{i}"][zi, zr : zr + 8] = part[ro : ro + 8, co : co + HEAD]
+            r[f"zs{i}"][zi, zr : zr + 8] = part[ro : ro + 8, co : co + HEAD].astype(BF)
         loop_z(lambda o: z_hop(i, o).start())
 
     def start_gather(i):
         loop_z(lambda o: z_hop(i, o).wait_recv())
-        t = r[f"zs{i}"][z]
+        t = r[f"zs{i}"][z].astype(F32)
         for o in range(1, Z):
-            t = t + r[f"zr{i}"][o]
-        r[f"zo{i}"][z] = t * ((Z * N * rows) ** -0.5)
+            t = t + r[f"zr{i}"][o].astype(F32)
+        r[f"zo{i}"][z] = (t * ((Z * N * rows) ** -0.5)).astype(r[f"zo{i}"].dtype)
         loop_z(lambda o: z_gather(i, o).start())
 
     def finish(i):
         loop_z(lambda o: z_gather(i, o).wait_recv())
         for zi, zr, ro, co in tiles_of(i):
-            val = r[f"zo{i}"][zi, zr : zr + 8]
+            val = r[f"zo{i}"][zi, zr : zr + 8].astype(F32)
             if i == 0:
                 gq_ref[ro : ro + 8, co : co + HEAD] = val
             elif co < p.kv_cols:
@@ -618,6 +597,7 @@
     mark("grads4", grads, 4)
     mark("ret4", lambda: [ret4(g) for g in range(G)])
     mark("grads2", grads, 2)
+    mark("ret2", lambda: [ret2(g) for g in range(G)])
     mark("grads0", grads, 0)
 
     def dq_rows():
@@ -628,32 +608,31 @@
     mark("dq_rows", dq_rows)
     dq_copy = remote(r["dq"], r["dqp"], *pair("dq"), peer)
     dq_copy.start()
-    mark("w_dq", lambda: (tokt_copy.wait_recv(), dq_copy.wait_recv()))
-    mark("made_q", made_q, 0)
-    one[0][0].start_up()
-    mark("fwd_far", lambda: [forward_far(g) for g in range(G)])
-    mark("ret2_0", ret2, 0)
-    mark("made_q", made_q, 1)
-    one[0][1].start_up()
-    mark("ret2_1", ret2, 1)
-
     def gi_q(n, c):
         at = pl.ds(pl.multiple_of(n * step, step), step)
         r["gi32"][:, at] = nt(r["dq"][...], r["wq"][at])
         return c
 
     mark("gi_q", lax.fori_loop, 0, p.width // step, gi_q, 0)
+    mark("fwd_far", lambda: [forward_far(0, i) for i in range(2)])
+    mark("w_dq", lambda: (tokt_copy.wait_recv(), dq_copy.wait_recv()))
+    mark("made_q", made_q, 0)
+    one[0][0].two_up().start()
+    mark("fwd_far2", forward_far, 1, 0)
+    mark("made_q", made_q, 1)
+    one[0][1].two_up().start()
+    mark("fwd_far2", forward_far, 1, 1)
+
+    mark("pass_q", one[0][0].pass_up)
     mark("ret0_0", ret0, 0)
-    mark("pass_q", one[0][0].pass_up)
-    one[0][0].start_down()
+    one[0][0].down().start()
     mark("ret0_1", ret0, 1)
+    one[0][1].down().start()
     mark("pass_q", one[0][1].pass_up)
-    one[0][1].start_down()
     mark("w_dkv", lambda: [dkv_copy(g).wait_recv() for g in range(G)])
     for j in range(2):
         mark("made_kv", made_kv, j)
-        one[1][j].start_up()
-        one[1][j].start_down()
+        one[1][j].start()
 
     def gi_kv(n, c):
         at = pl.ds(pl.multiple_of(n * step, step), step)
@@ -664,12 +643,9 @@
         gi_ref[:, at] = val.astype(BF)
         return c
 
+    mark("second_0", start_second, 0)
     mark("gi_kv", lax.fori_loop, 0, p.width // step, gi_kv, 0)
-    mark("pass_kv", lambda: [f() for j in range(2) for f in (one[1][j].pass_up, one[1][j].pass_down)])
-    mark("second_0", start_second, 0)
     mark("second_1", start_second, 1)
-    mark("pass2_0", pass_second, 0)
-    mark("pass2_1", pass_second, 1)
     mark("z_0", start_z, 0)
     mark("z_1", start_z, 1)
     mark("gather_0", start_gather, 0)
@@ -684,8 +660,11 @@
     for copy in (h_one(0), h_three(2), far_one, far_two, tokt_copy, dq_copy):
         copy.wait_send()
     for g in range(G):
-        for copy in (ret(g, 3, peer), ret(g, 1, peer), ret(g, 2, prv), ret_four(g), far_send(g), far_last(g), dkv_copy(g)):
+        for copy in (ret(g, 3, peer), ret(g, 1, peer), ret(g, 2, prv), dkv_copy(g)):
             copy.wait_send()
+    for unit in units:
+        far_send(*unit).wait_send()
+        far_last(*unit).wait_send()
     for i in range(2):
         for ring_sum in one[i] + two[i]:
             for copy in ring_sum.copies():

time: 86.8 us -> 78.3 us (0.902)
  Pallas kernels: 85.4 us -> 77.1 us
    pallas_call x1, Pallas kernels: 83.4 us -> 75.1 us  [body(): pl.pallas_call(functools.partial(kernel, p), out_shape=shapes, in_specs=[...]
where the time goes in v3:
time: 78.3 us; the launch traced here: 77.8 us
  Pallas kernels  77.1 us (98%)
    pallas_call x1, Pallas kernels, body(): pl.pallas_call(functools.partial(kernel, p), out_shape=shapes, in_specs=[...  75.1 us
    pallas_call x1, Pallas kernels, body(): pl.pallas_call(emit, out_shape=shapes, in_specs=[vmem] * 4, out_specs=(an...  2 us

profile of v3, /device:TPU:24, one launch (start us, length us, event | category | flops | bytes accessed | tf_op | source)
XLA Modules:
  0.0 77.8 jit_solution(6272688054172156039)
XLA Ops:
  0.6 75.1 %step.1 = (bf16[256,1024]{1,0:T(8,128)(2,1)}, f32[32,1024]{1,0:T(8,128)}, f32[32,256]{1,0:T(8,128)}, f32[32,256]{1,0:T(8,128)}) custom-call(bf16[256,1024]{1,0:T(8,128)(2,1)} %bitcast.3, bf16[1024,1024]{1,0:T(8,128)(2,1)} %wq_h.1, bf16[1024,256]{1,0:T(8,128)(2,1)} %wk_h.1, bf16[1024,256]{1,0:T(8,128)(2,1)} %wv_h.1, bf16[256,1024]{1,0:T(8,128)(2,1)} %bitcast.4, ...), custom_call_target="tpu_custom_call" | custom-call | tf_op jit(solution)/shard_map/step/pallas_call | solution.py:697
  75.8 2.0 %emit.1 = (bf16[256,1024]{1,0:T(8,128)(2,1)}, f32[32,1024]{1,0:T(8,128)}, f32[32,256]{1,0:T(8,128)}, f32[32,256]{1,0:T(8,128)}) custom-call(bf16[256,1024]{1,0:T(8,128)(2,1)} %get-tuple-element.12.refs_0_, f32[32,1024]{1,0:T(8,128)} %get-tuple-element.13.refs_1_, f32[32,256]{1,0:T(8,128)} %get-tuple-element.14.refs_2_, f32[32,256]{1,0:T(8,128)} %get-tuple-element.15.refs_3_), custom_call_target="tpu_custom_call" | custom-call | tf_op jit(solution)/shard_map/emit/pallas_call | solution.py:708

commit v4 on v3

--- a/solution.py
+++ b/solution.py
@@ -555,6 +555,10 @@
 
         lax.fori_loop(0, Z - 1, body, 0)
 
+    def each_z(f):
+        for o in range(1, Z):
+            f(o)
+
     def tiles_of(i):
         per_z = r[f"zs{i}"].shape[1] // 8
         ncb = sum(c for _, c, _ in p.parts[i]) // HEAD
@@ -571,7 +575,7 @@
         loop_z(lambda o: z_hop(i, o).start())
 
     def start_gather(i):
-        loop_z(lambda o: z_hop(i, o).wait_recv())
+        each_z(lambda o: z_hop(i, o).wait_recv())
         t = r[f"zs{i}"][z].astype(F32)
         for o in range(1, Z):
             t = t + r[f"zr{i}"][o].astype(F32)
@@ -579,7 +583,7 @@
         loop_z(lambda o: z_gather(i, o).start())
 
     def finish(i):
-        loop_z(lambda o: z_gather(i, o).wait_recv())
+        each_z(lambda o: z_gather(i, o).wait_recv())
         for zi, zr, ro, co in tiles_of(i):
             val = r[f"zo{i}"][zi, zr : zr + 8].astype(F32)
             if i == 0:
@@ -648,29 +652,33 @@
     mark("second_1", start_second, 1)
     mark("z_0", start_z, 0)
     mark("z_1", start_z, 1)
+
+    def sent_1():
+        for u in range(both):
+            h_next(u).wait_send()
+        for u in range(G):
+            h_four(u).wait_send()
+        for copy in (h_one(0), h_three(2), far_one, far_two, tokt_copy, dq_copy):
+            copy.wait_send()
+        for g in range(G):
+            for copy in (ret(g, 3, peer), ret(g, 1, peer), ret(g, 2, prv), dkv_copy(g)):
+                copy.wait_send()
+        for unit in units:
+            far_send(*unit).wait_send()
+            far_last(*unit).wait_send()
+        for i in range(2):
+            for ring_sum in one[i] + two[i]:
+                for copy in ring_sum.copies():
+                    copy.wait_send()
+
+    mark("sent_1", sent_1)
     mark("gather_0", start_gather, 0)
     mark("gather_1", start_gather, 1)
+    mark("sent_2", lambda: [each_z(lambda o, i=i: z_hop(i, o).wait_send()) for i in range(2)])
     mark("finish_0", finish, 0)
     mark("finish_1", finish, 1)
 
-    for u in range(both):
-        h_next(u).wait_send()
-    for u in range(G):
-        h_four(u).wait_send()
-    for copy in (h_one(0), h_three(2), far_one, far_two, tokt_copy, dq_copy):
-        copy.wait_send()
-    for g in range(G):
-        for copy in (ret(g, 3, peer), ret(g, 1, peer), ret(g, 2, prv), dkv_copy(g)):
-            copy.wait_send()
-    for unit in units:
-        far_send(*unit).wait_send()
-        far_last(*unit).wait_send()
-    for i in range(2):
-        for ring_sum in one[i] + two[i]:
-            for copy in ring_sum.copies():
-                copy.wait_send()
-        loop_z(lambda o: z_hop(i, o).wait_send())
-        loop_z(lambda o: z_gather(i, o).wait_send())
+    mark("sent_3", lambda: [each_z(lambda o, i=i: z_gather(i, o).wait_send()) for i in range(2)])
 
 
 def emit(*refs):

time: 78.3 us -> 77.3 us (0.987)
  Pallas kernels: 77.1 us -> 76.1 us
    pallas_call x1, Pallas kernels: 75.1 us -> 74.1 us  [body(): pl.pallas_call(functools.partial(kernel, p), out_shape=shapes, in_specs=[...]
where the time goes in v4:
time: 77.3 us; the launch traced here: 76.7 us
  Pallas kernels  76.1 us (98%)
    pallas_call x1, Pallas kernels, body(): pl.pallas_call(functools.partial(kernel, p), out_shape=shapes, in_specs=[...  74.1 us
    pallas_call x1, Pallas kernels, body(): pl.pallas_call(emit, out_shape=shapes, in_specs=[vmem] * 4, out_specs=(an...  2 us

profile of v4, /device:TPU:24, one launch (start us, length us, event | category | flops | bytes accessed | tf_op | source)
XLA Modules:
  0.0 76.7 jit_solution(12564730570008866591)
XLA Ops:
  0.6 74.1 %step.1 = (bf16[256,1024]{1,0:T(8,128)(2,1)}, f32[32,1024]{1,0:T(8,128)}, f32[32,256]{1,0:T(8,128)}, f32[32,256]{1,0:T(8,128)}) custom-call(bf16[256,1024]{1,0:T(8,128)(2,1)} %bitcast.3, bf16[1024,1024]{1,0:T(8,128)(2,1)} %wq_h.1, bf16[1024,256]{1,0:T(8,128)(2,1)} %wk_h.1, bf16[1024,256]{1,0:T(8,128)(2,1)} %wv_h.1, bf16[256,1024]{1,0:T(8,128)(2,1)} %bitcast.4, ...), custom_call_target="tpu_custom_call" | custom-call | tf_op jit(solution)/shard_map/step/pallas_call | solution.py:705
  74.7 2.0 %emit.1 = (bf16[256,1024]{1,0:T(8,128)(2,1)}, f32[32,1024]{1,0:T(8,128)}, f32[32,256]{1,0:T(8,128)}, f32[32,256]{1,0:T(8,128)}) custom-call(bf16[256,1024]{1,0:T(8,128)(2,1)} %get-tuple-element.12.refs_0_, f32[32,1024]{1,0:T(8,128)} %get-tuple-element.13.refs_1_, f32[32,256]{1,0:T(8,128)} %get-tuple-element.14.refs_2_, f32[32,256]{1,0:T(8,128)} %get-tuple-element.15.refs_3_), custom_call_target="tpu_custom_call" | custom-call | tf_op jit(solution)/shard_map/emit/pallas_call | solution.py:716
